TPU v7x, 512 devices: a whole 4x8x8 slice. The times are simulated.
512 devices in a mesh: pair: 64 (over z_hi, y, core), fft: 8 (over x, z_lo).
Axes of the slice: x: 4, y: 8, z: 8 (z_hi: 4, z_lo: 2; z = z_hi * 2 + z_lo), core: 2. Of those that a mesh axis runs over, the one named last changes fastest.
Arguments:
- psi_val: bfloat16 [384, 64, 64, 128], P('pair', 'fft'), may hold values from -6 to 6
- psi_cond: bfloat16 [384, 64, 64, 128], P('pair', 'fft'), may hold values from -6 to 6
- pair_bands: int32 [256, 2], P('pair'), may hold values from 0 to 5
- eps_val: float32 [384], P('pair'), may hold values from -4.125 to -0.125
- eps_cond: float32 [384], P('pair'), may hold values from 0.125 to 4.125
- g_map: int32 [10240], P('fft'), may hold values from 0 to 262143, as said below
Outputs:
- chi0: float32 [2, 10240, 10240], P(None, 'pair', 'fft')
Inputs may be any that keep to these rules, and one draw needn't show every extreme that they name: `pair_bands`: values name bands of the pair's own group. `g_map`: distinct values; the plane waves of block f (entries f * 1280 to (f + 1) * 1280 - 1) all lie on grid points whose second coordinate y is within f * 8 to (f + 1) * 8 - 1.
All inputs are finite; a program needn't handle non-finite values.
Results may differ from a plain program's by a relative error of at most 0.017.
Values may be sent and summed in bfloat16 or wider, within the bound.
No kernel may reach another device: no remote copies, remote signals or barrier semaphores. Data moves between devices by JAX's collectives and lax.ppermute only.
A program may use at most 64 MiB of HBM per device.

v0:
```python
import math

import jax
import jax.numpy as jnp
from jax import lax
from jax.sharding import PartitionSpec as P

NG = 10240


table_mode = lax.Precision.HIGH


def spread(value, axis, root):
    mine = lax.axis_index(axis) == root
    return lax.psum(jnp.where(mine, value, jnp.zeros_like(value)), axis)


def dft_tables(length):
    counter = jnp.arange(length, dtype=jnp.int32)
    angles = (counter[:, None] * counter[None, :] % length).astype(jnp.float32) * (
        2.0 * math.pi / length
    )
    factor = 1.0 / math.sqrt(length)
    return (jnp.cos(angles) * factor, jnp.sin(angles) * factor)


def along_last(values, cosine, sine_table):
    upper_rows = jnp.concatenate([cosine, -sine_table], axis=1)
    lower_rows = jnp.concatenate([sine_table, cosine], axis=1)
    matrix = jnp.concatenate([upper_rows, lower_rows], axis=0)
    return jnp.einsum("pxyc,cd->pxyd", values, matrix, precision=table_mode)


def along_inner(values, cosine, sine_table, pattern):
    direct = jnp.einsum(pattern, cosine, values, precision=table_mode)
    crossed = jnp.einsum(pattern, sine_table, values, precision=table_mode)
    middle = values.shape[-1] // 2
    swapped = jnp.concatenate([crossed[..., middle:], -crossed[..., :middle]], axis=-1)
    return direct + swapped


def owner_rows(columns, weights, row_count):
    block_width = columns.shape[2]
    start_col = lax.axis_index("pair") * row_count % block_width
    window = lax.dynamic_slice_in_dim(columns, start_col, row_count, 2)
    return (weights[:, None, None] * window.astype(jnp.float32)).astype(jnp.bfloat16)


def tile_product(scaled, columns):
    pair_count = scaled.shape[0]
    row_count = scaled.shape[2]
    turned = jnp.stack([-scaled[:, 1], scaled[:, 0]], axis=1)
    left_side = jnp.concatenate(
        [scaled.reshape(2 * pair_count, row_count), turned.reshape(2 * pair_count, row_count)],
        axis=1,
    )
    right_side = columns.reshape(2 * pair_count, columns.shape[2])
    product = lax.dot_general(
        left_side, right_side, (((0,), (0,)), ((), ())), preferred_element_type=jnp.float32
    )
    return product.reshape(2, row_count, columns.shape[2])


def on_device(psi_val, psi_cond, pair_bands, eps_val, eps_cond, g_map):
    band_count = psi_val.shape[0]
    grid_size = psi_val.shape[2]
    cosine, sine_table = dft_tables(grid_size)
    band_ids = jnp.arange(band_count, dtype=jnp.int32)[None, :]
    choose_valence = pair_bands[:, 0:1] == band_ids
    choose_conduction = pair_bands[:, 1:2] == band_ids
    valence_field = jnp.einsum(
        "pb,bxyc->pxyc",
        choose_valence.astype(jnp.bfloat16),
        psi_val,
        preferred_element_type=jnp.float32,
    )
    conduction_field = jnp.einsum(
        "pb,bxyc->pxyc",
        choose_conduction.astype(jnp.bfloat16),
        psi_cond,
        preferred_element_type=jnp.float32,
    )
    valence_re = valence_field[..., :grid_size]
    valence_im = valence_field[..., grid_size:]
    conduction_re = conduction_field[..., :grid_size]
    conduction_im = conduction_field[..., grid_size:]
    density = jnp.concatenate(
        [
            valence_re * conduction_re + valence_im * conduction_im,
            valence_re * conduction_im - valence_im * conduction_re,
        ],
        axis=-1,
    )
    valence_energy = jnp.sum(choose_valence.astype(jnp.float32) * eps_val[None, :], axis=1)
    conduction_energy = jnp.sum(choose_conduction.astype(jnp.float32) * eps_cond[None, :], axis=1)
    weight = 2.0 / (valence_energy - conduction_energy)
    transformed = along_last(density, cosine, sine_table)
    transformed = along_inner(transformed, cosine, sine_table, "kn,pxnc->pxkc")
    slab_rows = grid_size // lax.axis_size("fft")
    x_index = g_map // (grid_size * grid_size)
    y_index = g_map // grid_size % grid_size - lax.axis_index("fft") * slab_rows
    z_index = g_map % grid_size
    position = (x_index * slab_rows + y_index) * (2 * grid_size) + z_index
    spectrum = along_inner(
        lax.all_to_all(
            transformed.astype(jnp.bfloat16), "fft", split_axis=2, concat_axis=1, tiled=True
        ).astype(transformed.dtype),
        cosine,
        sine_table,
        "kn,pnyc->pkyc",
    )
    flattened = spectrum.reshape(spectrum.shape[0], -1)
    real_part = jnp.take(flattened, position, axis=1)
    imag_part = jnp.take(flattened, position + grid_size, axis=1)
    elements = jnp.stack([real_part, imag_part], axis=1).astype(jnp.bfloat16)
    row_count = NG // lax.axis_size("pair")
    owner_index = lax.axis_index("pair") * row_count // g_map.shape[0]
    columns, weights = (
        lax.all_gather(elements, "pair", axis=0, tiled=True),
        lax.all_gather(weight.astype(jnp.bfloat16), "pair", axis=0, tiled=True).astype(
            weight.dtype
        ),
    )
    scaled = spread(owner_rows(columns, weights, row_count), "fft", owner_index)
    accumulated = tile_product(scaled, columns)
    return accumulated * (1.0 / (weight.shape[0] * lax.axis_size("pair")))


def solution(mesh):
    in_specs = (
        P("pair", "fft", None, None),
        P("pair", "fft", None, None),
        P("pair", None),
        P("pair"),
        P("pair"),
        P("fft"),
    )
    out_specs = P(None, "pair", "fft")
    return jax.shard_map(
        on_device, mesh=mesh, in_specs=in_specs, out_specs=out_specs, check_vma=False
    )
```

profile of v0, /device:TPU:9, one launch (start us, length us, event | category | flops | bytes accessed | tf_op | source)
XLA Modules:
  0.0 300.5 jit_solution(16423472887477996348)
XLA Ops:
  6.5 0.0 copy-start
  6.5 0.0 copy-start.2
  6.5 0.2 sine_multiply_fusion
  6.7 0.1 fusion.31
  6.8 0.9 slice_bitcast_fusion.1
  7.7 0.0 copy-done
  7.7 0.7 fusion.5
  8.4 0.0 copy-done.2
  8.4 0.7 fusion.7
  9.0 1.1 multiply_add_fusion
  10.2 0.6 pad_maximum_fusion
  10.8 0.6 fusion.3
  11.5 0.7 convolution_bitcast_fusion.2
  12.2 0.4 fusion.70
  12.6 0.9 fusion.2
  13.5 0.0 copy-start.3
  13.5 1.1 copy.38
  14.6 5.8 %all-to-all-start = ((bf16[4,8,64,128]{3,1,0,2:T(8,128)(2,1)}), bf16[4,8,64,128]{3,1,0,2:T(8,128)(2,1)S(1)}, u32[]{:S(2)}, u32[]{:S(2)}) async-start(bf16[4,8,64,128]{3,1,0,2:T(8,128)(2,1)} %copy.38), calls=%async_computation | async-start | bytes 1048576 | tf_op jit(solution)/shard_map/all_to_all | solution.py:106
  20.5 0.2 all-gather.2.cloned.1.call-start
  20.7 0.0 copy-done.3
  20.8 8.9 %all-to-all-done = bf16[4,8,64,128]{3,1,0,2:T(8,128)(2,1)S(1)} async-done(((bf16[4,8,64,128]{3,1,0,2:T(8,128)(2,1)}), bf16[4,8,64,128]{3,1,0,2:T(8,128)(2,1)S(1)}, u32[]{:S(2)}, u32[]{:S(2)}) %all-to-all-start) | async-done | bytes 524320 | tf_op jit(solution)/shard_map/all_to_all | solution.py:106
  29.7 0.5 convolution_bitcast_fusion
  30.2 0.4 fusion.69
  30.7 0.7 fusion.1
  31.4 12.0 %copy.50 = bf16[4,64,8,128]{0,3,2,1:T(8,128)(2,1)} copy(bf16[4,64,8,128]{3,1,2,0:T(8,128)(2,1)S(1)} %fusion.1) | data formatting | bytes 1048576 | tf_op jit(solution)/shard_map/reshape | solution.py:113
  43.4 10.3 %gather_fusion.1 = bf16[1280,4]{1,0:T(8,128)(2,1)S(1)} fusion(bf16[4,65536]{0,1:T(8,128)(2,1)} %bitcast.76, s32[2048]{0:T(1024)S(1)} %get-tuple-element.24), kind=kCustom, calls=%fused_computation.1.clone | custom fusion | bytes 25600 | tf_op jit(solution)/shard_map/jit(_take)/gather | solution.py:115
  53.7 10.3 %gather_fusion = bf16[1280,4]{1,0:T(8,128)(2,1)S(1)} fusion(bf16[4,65536]{0,1:T(8,128)(2,1)} %bitcast.77, s32[2048]{0:T(1024)S(1)} %get-tuple-element.25), kind=kCustom, calls=%fused_computation.clone | custom fusion | bytes 25600 | tf_op jit(solution)/shard_map/jit(_take)/gather | solution.py:114
  64.0 0.0 copy-start.4
  64.0 0.0 copy-start.5
  64.0 0.2 fusion.14
  64.3 0.2 fusion.13
  64.5 0.1 pad_maximum_fusion.1
  64.7 0.9 copy.43
  65.5 0.0 all-gather.2.cloned.1.call-update
  65.5 0.0 all-reduce.3.cloned.1.call-start
  65.6 1.3 dynamic-slice
  67.6 0.0 copy-done.4
  67.6 0.0 copy-done.5
  67.6 0.2 select_reduce_fusion
  67.8 0.2 dynamic-update-slice
  68.1 139.1 %all-reduce = bf16[256]{0:T(256)(128)(2,1)S(1)} all-reduce(bf16[256]{0:T(256)(128)(2,1)S(1)} %dynamic-update-slice), channel_id=1, replica_groups=mesh['pair'=64,'fft'=8] {'pair'}, use_global_device_ids=true, to_apply=%add | all-reduce | flops 256 | bytes 1024
  207.2 0.0 all-gather.2.cloned.1.call-done
  207.3 2.4 broadcast_select_fusion
  209.7 0.0 all-reduce.3.cloned.1.call-update
  209.7 3.2 %reshape.58 = bf16[512,1280,1]{1,0,2:T(8,128)(2,1)S(1)} reshape(bf16[256,2,1280]{2,1,0:T(2,128)(2,1)} %all-gather.2.cloned.1.call-done) | data formatting | bytes 2621440 | tf_op jit(solution)/shard_map/reshape | solution.py:58
  212.9 75.8 %all-reduce.3.cloned.1.call-done = bf16[256,2,160]{2,1,0:T(2,128)(2,1)} async-done(((bf16[256,2,160]{2,1,0:T(2,128)(2,1)}), bf16[256,2,160]{2,1,0:T(2,128)(2,1)}) %all-reduce.3.cloned.1.call-update) | async-done | bytes 163856 | tf_op jit(solution)/shard_map/psum | solution.py:16
  288.7 0.0 copy-start.1
  288.7 1.7 slice_negate_fusion.2
  290.4 0.7 pad_maximum_fusion.2
  291.1 0.2 reshape.24
  291.3 0.0 copy-done.1
  291.3 0.2 reshape.23
  291.6 0.1 maximum_bitcast_fusion
  291.7 0.2 copy.44
  291.9 1.8 convolution_multiply_fusion
  (7 shorter events, 0.1 us)
Async XLA Ops:
  6.5 1.2 copy-start
  6.5 1.8 copy-start.2
  13.5 7.2 %copy-start.3 = (s32[1280]{0:T(1024)S(1)}, s32[1280]{0:T(1024)}, u32[]{:S(2)}) copy-start(s32[1280]{0:T(1024)} %param.13) | copy-start | bytes 15364
  14.6 15.1 %all-to-all-start = ((bf16[4,8,64,128]{3,1,0,2:T(8,128)(2,1)}), bf16[4,8,64,128]{3,1,0,2:T(8,128)(2,1)S(1)}, u32[]{:S(2)}, u32[]{:S(2)}) async-start(bf16[4,8,64,128]{3,1,0,2:T(8,128)(2,1)} %copy.38), calls=%async_computation | async-start | bytes 1048576 | tf_op jit(solution)/shard_map/all_to_all | solution.py:106
  20.5 186.8 %all-gather.2.cloned.1.call-start = ((), (), s32[]{:S(2)}) async-start(), calls=%async_computation.1 | async-start | bytes 1331200 | tf_op jit(solution)/shard_map/all_gather | solution.py:120
  64.0 3.6 %copy-start.4 = (f32[6]{0:T(128)S(1)}, f32[6]{0:T(128)}, u32[]{:S(2)}) copy-start(f32[6]{0:T(128)} %param.12) | copy-start | bytes 76
  64.0 3.6 %copy-start.5 = (f32[6]{0:T(128)S(1)}, f32[6]{0:T(128)}, u32[]{:S(2)}) copy-start(f32[6]{0:T(128)} %param.11) | copy-start | bytes 76
  65.5 223.2 %all-reduce.3.cloned.1.call-start = ((), (), s32[]{:S(2)}) async-start(), calls=%async_computation.2 | async-start | bytes 524288 | tf_op jit(solution)/shard_map/psum | solution.py:16
  288.7 2.6 copy-start.1
Sparse Core Ops, SparseCore 0:
  65.7 85.6 all-gather.1
  209.8 78.8 all-reduce.2
where the time goes:
time: 306 us; the launch traced here: 301 us
  blocking collectives  139 us (45%)
  waiting for transfers between devices  84.8 us (28%)
  local copies, waits for them, and re-layouts  40.9 us (13%)
  between operations  14.4 us (5%)
  other arithmetic  8.67 us (3%)
  matrix products  6.59 us (2%)
  starting transfers between devices  6.09 us (2%)
    unnamed x1, blocking collectives  139 us
    psum x1, waiting for transfers between devices, spread(): return lax.psum(jnp.where(mine, value, jnp.zeros_like(value)), axis)  75.8 us
    reshape x1, local copies, waits for them, and re-layouts, on_device(): flattened = spectrum.reshape(spectrum.shape[0], -1)  12 us
    gather x1, local copies, waits for them, and re-layouts, on_device(): real_part = jnp.take(flattened, position, axis=1)  10.3 us
    gather x1, local copies, waits for them, and re-layouts, on_device(): imag_part = jnp.take(flattened, position + grid_size, axis=1)  10.3 us
    all_to_all x1, waiting for transfers between devices, on_device(): lax.all_to_all(transformed.astype(jnp.bfloat16), 'fft', split_axis=2, con...  8.91 us
  transfers between devices with their start and end apart: 3, of which 2 were waited for; matrix products, arithmetic and copies ran while one was open for 2% of the time, Pallas kernels for 0%

commit v1 on v0

v1 whole, which is shorter than its diff:
```python
import math

import jax
import jax.numpy as jnp
import numpy as np
from jax import lax
from jax.experimental import pallas as pl
from jax.experimental.pallas import tpu as pltpu
from jax.sharding import Mesh
from jax.sharding import PartitionSpec as P

N = 64
G_BLK = 1280
PAIRS = 256
ROWS = 160
MSG = 1664
F32 = jnp.float32
BF16 = jnp.bfloat16


def host_tables():
    k = np.arange(N)
    angle = 2.0 * math.pi * ((k[:, None] * k[None, :]) % N) / N
    c, s = np.cos(angle), np.sin(angle)
    top = np.concatenate([c, -s, -s, -c], axis=1)
    low = np.concatenate([s, c, c, -s], axis=1)
    z_table = np.concatenate([top, top, low, -low], axis=0)
    order = np.concatenate([k[0::2], k[1::2]])
    y_table = np.concatenate([c, s], axis=1)[order]
    to_re = np.stack([c, s], axis=1).reshape(2 * N, N)
    to_im = np.stack([-s, c], axis=1).reshape(2 * N, N)
    x_table = np.concatenate([to_re, to_im], axis=0)
    return z_table, y_table, x_table


def two_parts(table, axis):
    kind = np.dtype(BF16)
    high = table.astype(kind)
    return np.concatenate([high, (table - high.astype(np.float64)).astype(kind)], axis=axis)


def local_dft_kernel(bands, val, cond, z_tab, y_tab, out, scratch):
    del bands
    v = val[0].astype(F32).reshape(8 * N, 2 * N)
    c = cond[0].astype(F32).reshape(8 * N, 2 * N)
    products = jnp.concatenate([v * c, v * pltpu.roll(c, N, 1)], axis=1).astype(BF16)
    both = jnp.dot(products, z_tab[...], preferred_element_type=F32)
    along_z = (both[:, : 4 * N] + both[:, 4 * N :]).astype(BF16)
    parts = []
    for x in range(8):
        rows = along_z[x * N : (x + 1) * N]
        parts.append(jnp.concatenate([rows[:, : 2 * N], rows[:, 2 * N :]] * 2, axis=0))
    along_y = jnp.dot(y_tab[...], jnp.concatenate(parts, axis=1), preferred_element_type=F32)
    first = lax.broadcasted_iota(jnp.int32, (N // 2, 2 * N), 1) < N
    for x in range(8):
        tile = along_y[:, x * 2 * N : (x + 1) * 2 * N]
        even, odd = tile[: N // 2], tile[N // 2 :]
        scratch[pl.ds(x * N, N // 2), :] = jnp.where(first, even, pltpu.roll(odd, N, 1))
        scratch[pl.ds(x * N + N // 2, N // 2), :] = jnp.where(first, pltpu.roll(even, N, 1), odd)
    for k in range(N // 2):
        out[k // 4, k % 4] = scratch[pl.ds(k, 16, stride=N // 2), :].astype(BF16)


def local_dft(pair_bands, psi_val, psi_cond, z_tab, y_tab):
    band = lambda which: pl.BlockSpec((1, 8, N, 2 * N), lambda i, b: (b[i, which], 0, 0, 0))
    whole = lambda shape: pl.BlockSpec(shape, lambda i, b: (0, 0))
    return pl.pallas_call(
        local_dft_kernel,
        grid_spec=pltpu.PrefetchScalarGridSpec(
            num_scalar_prefetch=1,
            grid=(4,),
            in_specs=[band(0), band(1), whole(z_tab.shape), whole(y_tab.shape)],
            out_specs=pl.BlockSpec((8, 4, 16, 2 * N), lambda i, b: (0, 0, i, 0)),
            scratch_shapes=[pltpu.VMEM((8 * N, 2 * N), F32)],
        ),
        out_shape=jax.ShapeDtypeStruct((8, 4, N, 2 * N), BF16),
        name="local_dft",
    )(pair_bands, psi_val, psi_cond, z_tab, y_tab)


def picks_kernel(g_map, x_tab, column_pick, twiddle):
    g = g_map[...]
    row = lax.broadcasted_iota(jnp.int32, (8 * N, G_BLK), 0)
    column_pick[...] = jnp.where(row == (g & (8 * N - 1)), 1.0, 0.0).astype(BF16)
    row = lax.broadcasted_iota(jnp.int32, (2 * N, G_BLK), 0)
    x_pick = jnp.where((row & (N - 1)) == (g >> 12), 1.0, 0.0).astype(BF16)
    twiddle[...] = jnp.dot(x_tab[...], x_pick, preferred_element_type=F32)


def picks(g_map, x_tab):
    return pl.pallas_call(
        picks_kernel,
        out_shape=(
            jax.ShapeDtypeStruct((8 * N, G_BLK), BF16),
            jax.ShapeDtypeStruct((4 * N, G_BLK), F32),
        ),
        name="picks",
    )(g_map, x_tab)


def elements_kernel(bands, e_val, e_cond, slabs, column_pick, twiddle, elements, scaled):
    step = 256
    row = lax.broadcasted_iota(jnp.int32, (8, step), 0) % 4
    gap = jnp.zeros((8, step), F32)
    for i in range(4):
        gap = jnp.where(row == i, e_val[bands[i, 0]] - e_cond[bands[i, 1]], gap)
    weight = 2.0 / gap
    left = jnp.concatenate([slabs[:, s].reshape(8 * N, 2 * N) for s in range(4)], axis=1)
    for n in range(G_BLK // step):
        cols = pl.ds(n * step, step)
        picked = jnp.dot(left, column_pick[:, cols], preferred_element_type=F32)
        picked = picked.reshape(8, 4, 16, step)
        halves = []
        for h in range(2):
            factor = twiddle[pl.ds(h * 2 * N, 2 * N), cols].reshape(8, 1, 16, step)
            halves.append(jnp.sum(jnp.sum(picked * factor, axis=0), axis=1))
        values = (jnp.concatenate(halves, axis=0) * (1.0 / (N * 8))).astype(BF16)
        elements[:, cols] = values
        weighted = (weight * values.astype(F32)).astype(BF16)
        for f in range(8):
            scaled[f, :, cols] = weighted


def make_elements(pair_bands, eps_val, eps_cond, slabs, column_pick, twiddle):
    smem = pl.BlockSpec(memory_space=pltpu.SMEM)
    vmem = pl.BlockSpec(memory_space=pltpu.VMEM)
    return pl.pallas_call(
        elements_kernel,
        in_specs=[smem] * 3 + [vmem] * 3,
        out_shape=(
            jax.ShapeDtypeStruct((8, G_BLK), BF16),
            jax.ShapeDtypeStruct((8, 8, G_BLK), BF16),
        ),
        name="elements",
    )(pair_bands, eps_val, eps_cond, slabs, column_pick, twiddle)


def messages_kernel(core, elements, scaled, out):
    swapped = core[0] == 1
    values = elements[...]
    pad = jnp.zeros((8, MSG - G_BLK - 2 * ROWS), F32)
    for j in range(32):
        out[j, :, pl.ds(0, G_BLK)] = values
        part = (j % 4) * 2 * ROWS
        rows = scaled[j // 4].astype(F32)[:, part : part + 2 * ROWS]
        first, second = rows[:, :ROWS], rows[:, ROWS:]
        mine = jnp.where(swapped, second, first)
        other = jnp.where(swapped, first, second)
        out[j, :, pl.ds(G_BLK, MSG - G_BLK)] = jnp.concatenate([mine, pad, other], axis=1).astype(BF16)


def make_messages(core, elements, scaled):
    smem = pl.BlockSpec(memory_space=pltpu.SMEM)
    vmem = pl.BlockSpec(memory_space=pltpu.VMEM)
    return pl.pallas_call(
        messages_kernel,
        in_specs=[smem, vmem, vmem],
        out_shape=jax.ShapeDtypeStruct((32, 8, MSG), BF16),
        name="messages",
    )(core, elements, scaled)


def product_kernel(mine_rows, other_rows, mine_cols, other_cols, out, left):
    @pl.when(pl.program_id(0) == 0)
    def _():
        shift = MSG - G_BLK - ROWS
        a = mine_rows[...].astype(F32)
        b = pltpu.roll(other_rows[...].astype(F32), MSG - G_BLK - shift, 1)
        rows = jnp.concatenate([a[:, :256], b[:, :256]], axis=0)
        turned = pltpu.roll(rows.reshape(64, 8, 256), 4, 1)
        sign = jnp.where(lax.broadcasted_iota(jnp.int32, (64, 8, 256), 1) < 4, -1.0, 1.0)
        turned = (turned * sign).reshape(512, 256)
        left[pl.ds(0, ROWS), :] = rows.T[:ROWS].astype(BF16)
        left[pl.ds(ROWS, ROWS), :] = turned.T[:ROWS].astype(BF16)

    right = jnp.concatenate([mine_cols[...], other_cols[...]], axis=0)
    result = jnp.dot(left[...], right, preferred_element_type=F32) * (1.0 / PAIRS)
    out[0] = result[:ROWS]
    out[1] = result[ROWS:]


def product(mine, other):
    step = 256
    tail = MSG - G_BLK
    mine, other = mine.reshape(256, MSG), other.reshape(256, MSG)
    rows_m, rows_o = mine[:, G_BLK:], other[:, G_BLK:]
    cols = pl.BlockSpec((256, step), lambda n: (0, n))
    rows = pl.BlockSpec((256, tail), lambda n: (0, 0))
    return pl.pallas_call(
        product_kernel,
        grid=(G_BLK // step,),
        in_specs=[rows, rows, cols, cols],
        out_specs=pl.BlockSpec((2, ROWS, step), lambda n: (0, 0, n)),
        out_shape=jax.ShapeDtypeStruct((2, ROWS, G_BLK), F32),
        scratch_shapes=[pltpu.VMEM((2 * ROWS, 512), BF16)],
        name="product",
    )(rows_m, rows_o, mine, other)


def on_device(psi_val, psi_cond, pair_bands, eps_val, eps_cond, g_map):
    z_table, y_table, x_table = host_tables()
    z_tab = jnp.asarray(two_parts(z_table, 1))
    y_tab = jnp.asarray(two_parts(y_table, 1))
    x_tab = jnp.asarray(two_parts(x_table, 1))
    slabs = local_dft(pair_bands, psi_val, psi_cond, z_tab, y_tab)
    slabs = lax.all_to_all(slabs, ("x", "zl"), 0, 0, tiled=True)
    column_pick, twiddle = picks(g_map.reshape(1, G_BLK), x_tab)
    elements, scaled = make_elements(pair_bands, eps_val, eps_cond, slabs, column_pick, twiddle)
    scaled = lax.all_to_all(scaled, ("x", "zl"), 0, 0, tiled=True)
    core = lax.axis_index("core").astype(jnp.int32).reshape(1)
    mine = lax.all_to_all(make_messages(core, elements, scaled), ("zh", "y"), 0, 0, tiled=True)
    other = lax.ppermute(mine, "core", [(0, 1), (1, 0)])
    return product(mine, other)


def solution(mesh):
    fine = Mesh(mesh.devices.reshape(4, 8, 2, 4, 2), ("zh", "y", "core", "x", "zl"))
    pair, fft = ("zh", "y", "core"), ("x", "zl")
    in_specs = (
        P(pair, fft, None, None),
        P(pair, fft, None, None),
        P(pair, None),
        P(pair),
        P(pair),
        P(fft),
    )
    return jax.shard_map(
        on_device, mesh=fine, in_specs=in_specs, out_specs=P(None, pair, fft), check_vma=False
    )
```

time: 306 us -> 92.5 us (0.30); the launches traced: 301 us -> 91.9 us
  blocking collectives: 139 us -> 38.3 us
  waiting for transfers between devices: 84.8 us -> 12.7 us
  local copies, waits for them, and re-layouts: 40.9 us -> 5.1 us
  Pallas kernels: 0 us -> 19.7 us
  between operations: 14.4 us -> 0.04 us
  starting transfers between devices: 6.09 us -> 16 us
  other arithmetic: 8.67 us -> 0 us
  matrix products: 6.59 us -> 0 us
    unnamed x1 -> x0, blocking collectives: 139 us -> none
    psum x1 -> x0, waiting for transfers between devices: 75.8 us -> none  [spread(): return lax.psum(jnp.where(mine, value, jnp.zeros_like(value)), axis)]
    all_to_all x0 -> x1, blocking collectives: none -> 38.3 us  [on_device(): lax.all_to_all(make_messages(core, elements, scaled), ('zh', 'y'), 0, 0,...]
    gather x2 -> x0, local copies, waits for them, and re-layouts: 20.6 us -> none  [the longest x1 10.3 us: on_device(): real_part = jnp.take(flattened, position, axis=1)]
    pallas_call x0 -> x5, Pallas kernels: none -> 19.7 us  [the longest x1 5.88 us: local_dft(): pl.pallas_call(local_dft_kernel, grid_spec=pltpu.PrefetchScalarGridSpec(n...]
    reshape x4 -> x1, local copies, waits for them, and re-layouts: 15.6 us -> 0.59 us  [on_device(): column_pick, twiddle = picks(g_map.reshape(1, G_BLK), x_tab)]
    ppermute x0 -> x1, starting transfers between devices: none -> 6.8 us  [on_device(): other = lax.ppermute(mine, 'core', [(0, 1), (1, 0)])]
    dot_general x8 -> x0, matrix products: 6.59 us -> none  [the longest x1 1.76 us: tile_product(): lax.dot_general(left_side, right_side, (((0,), (0,)), ((), ())), preferre...]
  transfers between devices with their start and end apart: 3 -> 3, of which waited for: 2 -> 3; matrix products, arithmetic and copies ran while one was open for 2% -> 1% of each run, Pallas kernels for 0% -> 3%
where the time goes in v1:
time: 92.5 us; the launch traced here: 91.9 us
  blocking collectives  38.3 us (41%)
  Pallas kernels  19.7 us (21%)
  starting transfers between devices  16 us (17%)
  waiting for transfers between devices  12.7 us (14%)
  local copies, waits for them, and re-layouts  5.1 us (6%)
    all_to_all x1, blocking collectives, on_device(): lax.all_to_all(make_messages(core, elements, scaled), ('zh', 'y'), 0, 0,...  38.3 us
    ppermute x1, starting transfers between devices, on_device(): other = lax.ppermute(mine, 'core', [(0, 1), (1, 0)])  6.8 us
    pallas_call x1, Pallas kernels, local_dft(): pl.pallas_call(local_dft_kernel, grid_spec=pltpu.PrefetchScalarGridSpec(n...  5.88 us
    all_to_all x1, waiting for transfers between devices, on_device(): slabs = lax.all_to_all(slabs, ('x', 'zl'), 0, 0, tiled=True)  5.87 us
    all_to_all x1, starting transfers between devices, on_device(): slabs = lax.all_to_all(slabs, ('x', 'zl'), 0, 0, tiled=True)  5.83 us
    all_to_all x1, waiting for transfers between devices, on_device(): scaled = lax.all_to_all(scaled, ('x', 'zl'), 0, 0, tiled=True)  5.6 us
    pallas_call x1, Pallas kernels, product(): pl.pallas_call(product_kernel, grid=(G_BLK // step,), in_specs=[rows, row...  5.16 us
    pallas_call x1, Pallas kernels, make_elements(): pl.pallas_call(elements_kernel, in_specs=[smem] * 3 + [vmem] * 3, out_sha...  3.47 us
  transfers between devices with their start and end apart: 3, of which 3 were waited for; matrix products, arithmetic and copies ran while one was open for 1% of the time, Pallas kernels for 3%

profile of v1, /device:TPU:9, one launch (start us, length us, event | category | flops | bytes accessed | tf_op | source)
XLA Modules:
  0.0 91.9 jit_solution(7326439778121550900)
XLA Ops:
  0.0 1.3 %copy.11.bands = s32[4,2]{1,0:T(4,128)} copy(s32[4,2]{0,1:T(2,128)} %param.11) | data formatting | bytes 64 | tf_op args[2]
  1.3 0.0 copy-start.4
  1.4 5.9 %local_dft.1 = bf16[8,4,64,128]{3,2,1,0:T(8,128)(2,1)} custom-call(s32[4,2]{1,0:T(4,128)} %copy.11.bands, bf16[6,8,64,128]{3,2,1,0:T(8,128)(2,1)} %val.1, bf16[6,8,64,128]{3,2,1,0:T(8,128)(2,1)} %cond.1, bf16[256,512]{1,0:T(8,128)(2,1)} %constant.12.clone.z_tab, bf16[64,256]{1,0:T(8,128)(2,1)} %constant.13.clone.y_tab), custom_call_target="tpu_custom_call" | custom-call | tf_op jit(solution)/shard_map/local_dft/pallas_call | solution.py:67
  7.2 5.8 %all-to-all-start = ((bf16[8,4,64,128]{3,2,1,0:T(8,128)(2,1)}), bf16[8,4,64,128]{3,2,1,0:T(8,128)(2,1)S(1)}, u32[]{:S(2)}, u32[]{:S(2)}) async-start(bf16[8,4,64,128]{3,2,1,0:T(8,128)(2,1)} %local_dft.1), calls=%async_computation | async-start | bytes 1048576 | tf_op jit(solution)/shard_map/all_to_all | solution.py:206
  13.1 0.0 copy-done.4
  13.1 0.6 reshape.13.g_map
  13.7 2.7 %picks.1 = (bf16[512,1280]{1,0:T(8,128)(2,1)}, f32[256,1280]{1,0:T(8,128)}) custom-call(s32[1,1280]{1,0:T(1,128)} %reshape.13.g_map, bf16[256,128]{1,0:T(8,128)(2,1)} %constant.14.clone.x_tab), custom_call_target="tpu_custom_call" | custom-call | tf_op jit(solution)/shard_map/picks/pallas_call | solution.py:91
  16.4 5.9 %all-to-all-done.slabs = bf16[8,4,64,128]{3,2,1,0:T(8,128)(2,1)S(1)} async-done(((bf16[8,4,64,128]{3,2,1,0:T(8,128)(2,1)}), bf16[8,4,64,128]{3,2,1,0:T(8,128)(2,1)S(1)}, u32[]{:S(2)}, u32[]{:S(2)}) %all-to-all-start) | async-done | bytes 524320 | tf_op jit(solution)/shard_map/all_to_all | solution.py:206
  22.2 0.0 copy-start.1
  22.3 0.8 copy-done.1
  23.1 3.5 %elements.1 = (bf16[8,1280]{1,0:T(8,128)(2,1)}, bf16[8,8,1280]{2,1,0:T(8,128)(2,1)}) custom-call(s32[4,2]{1,0:T(4,128)} %copy.11.bands, f32[6]{0:T(128)} %e_val.1, f32[6]{0:T(128)} %e_cond.1, bf16[8,4,64,128]{3,2,1,0:T(8,128)(2,1)} %copy-done.1, bf16[512,1280]{1,0:T(8,128)(2,1)} %get-tuple-element.9.column_pick, f32[256,1280]{1,0:T(8,128)} %get-tuple-element.10.twiddle), custom_call_target="tpu_custom_call" | custom-call | tf_op jit(solution)/shard_map/elements/pallas_call | solution.py:127
  26.5 3.4 %all-to-all-start.1 = ((bf16[8,8,1280]{2,1,0:T(8,128)(2,1)}), bf16[8,8,1280]{2,1,0:T(8,128)(2,1)S(1)}, u32[]{:S(2)}, u32[]{:S(2)}) async-start(bf16[8,8,1280]{2,1,0:T(8,128)(2,1)} %get-tuple-element.12), calls=%async_computation.1 | async-start | bytes 327680 | tf_op jit(solution)/shard_map/all_to_all | solution.py:209
  29.9 5.6 %all-to-all-done.1.scaled = bf16[8,8,1280]{2,1,0:T(8,128)(2,1)S(1)} async-done(((bf16[8,8,1280]{2,1,0:T(8,128)(2,1)}), bf16[8,8,1280]{2,1,0:T(8,128)(2,1)S(1)}, u32[]{:S(2)}, u32[]{:S(2)}) %all-to-all-start.1) | async-done | bytes 163872 | tf_op jit(solution)/shard_map/all_to_all | solution.py:209
  35.5 0.0 copy-start.3
  35.5 0.7 copy-done.3
  36.2 2.5 %messages.1 = bf16[32,8,1664]{2,1,0:T(8,128)(2,1)} custom-call(s32[1]{0:T(128)} %bitcast.core, bf16[8,1280]{1,0:T(8,128)(2,1)} %get-tuple-element.11.elements, bf16[8,8,1280]{2,1,0:T(8,128)(2,1)} %copy-done.3), custom_call_target="tpu_custom_call" | custom-call | tf_op jit(solution)/shard_map/messages/pallas_call | solution.py:155
  38.6 38.3 %all_to_all.15 = bf16[32,8,1664]{2,1,0:T(8,128)(2,1)S(1)} all-to-all(bf16[32,8,1664]{2,1,0:T(8,128)(2,1)} %messages.1), channel_id=1, replica_groups=mesh['zh'=4,'y'=8,'core'=2,'x'=4,'zl'=2] {'zh','y'}, dimensions={0} | all-to-all | bytes 1703936 | tf_op jit(solution)/shard_map/all_to_all | solution.py:211
  76.9 0.0 copy-start
  76.9 6.8 %collective-permute-start = (bf16[32,8,1664]{2,1,0:T(8,128)(2,1)S(1)}, bf16[32,8,1664]{2,1,0:T(8,128)(2,1)S(1)}, u32[]{:S(2)}, u32[]{:S(2)}) collective-permute-start(bf16[32,8,1664]{2,1,0:T(8,128)(2,1)S(1)} %all_to_all.15), channel_id=1, source_target_pairs={{0,8},{8,0},{1,9},{9,1},{2,10},{10,2},{3,11},{11,3},{4,12},{12,4},... | collective-permute-start | bytes 2555912 | tf_op jit(solution)/shard_map/ppermute | solution.py:212
  83.7 0.7 slice.8.mine_rows
  84.4 1.3 %collective-permute-done = bf16[32,8,1664]{2,1,0:T(8,128)(2,1)S(1)} collective-permute-done((bf16[32,8,1664]{2,1,0:T(8,128)(2,1)S(1)}, bf16[32,8,1664]{2,1,0:T(8,128)(2,1)S(1)}, u32[]{:S(2)}, u32[]{:S(2)}) %collective-permute-start) | collective-permute-done | bytes 852000 | tf_op jit(solution)/shard_map/ppermute | solution.py:212
  85.7 0.0 copy-start.2
  85.7 0.7 slice.9.other_rows
  86.5 0.0 copy-done
  86.5 0.2 copy-done.2
  86.7 5.2 %product.1 = f32[2,160,1280]{2,1,0:T(8,128)} custom-call(bf16[256,384]{1,0:T(8,128)(2,1)} %slice.8.mine_rows, bf16[256,384]{1,0:T(8,128)(2,1)} %slice.9.other_rows, bf16[256,1664]{1,0:T(8,128)(2,1)} %bitcast.4, bf16[256,1664]{1,0:T(8,128)(2,1)} %bitcast.6), custom_call_target="tpu_custom_call" | custom-call | tf_op jit(solution)/shard_map/product/pallas_call | solution.py:189
Async XLA Ops:
  1.3 11.7 %copy-start.4 = (s32[1280]{0:T(1024)S(1)}, s32[1280]{0:T(1024)}, u32[]{:S(2)}) copy-start(s32[1280]{0:T(1024)} %param.14) | copy-start | bytes 15364
  7.2 15.0 %all-to-all-start = ((bf16[8,4,64,128]{3,2,1,0:T(8,128)(2,1)}), bf16[8,4,64,128]{3,2,1,0:T(8,128)(2,1)S(1)}, u32[]{:S(2)}, u32[]{:S(2)}) async-start(bf16[8,4,64,128]{3,2,1,0:T(8,128)(2,1)} %local_dft.1), calls=%async_computation | async-start | bytes 1048576 | tf_op jit(solution)/shard_map/all_to_all | solution.py:206
  22.2 0.8 copy-start.1
  26.5 9.0 %all-to-all-start.1 = ((bf16[8,8,1280]{2,1,0:T(8,128)(2,1)}), bf16[8,8,1280]{2,1,0:T(8,128)(2,1)S(1)}, u32[]{:S(2)}, u32[]{:S(2)}) async-start(bf16[8,8,1280]{2,1,0:T(8,128)(2,1)} %get-tuple-element.12), calls=%async_computation.1 | async-start | bytes 327680 | tf_op jit(solution)/shard_map/all_to_all | solution.py:209
  35.5 0.7 copy-start.3
  76.9 9.5 %copy-start = (bf16[32,8,1664]{2,1,0:T(8,128)(2,1)}, bf16[32,8,1664]{2,1,0:T(8,128)(2,1)S(1)}, u32[]{:S(2)}) copy-start(bf16[32,8,1664]{2,1,0:T(8,128)(2,1)S(1)} %all_to_all.15) | copy-start | bytes 2555908
  76.9 8.8 %collective-permute-start = (bf16[32,8,1664]{2,1,0:T(8,128)(2,1)S(1)}, bf16[32,8,1664]{2,1,0:T(8,128)(2,1)S(1)}, u32[]{:S(2)}, u32[]{:S(2)}) collective-permute-start(bf16[32,8,1664]{2,1,0:T(8,128)(2,1)S(1)} %all_to_all.15), channel_id=1, source_target_pairs={{0,8},{8,0},{1,9},{9,1},{2,10},{10,2},{3,11},{11,3},{4,12},{12,4},... | collective-permute-start | bytes 2555912 | tf_op jit(solution)/shard_map/ppermute | solution.py:212
  85.7 1.0 %copy-start.2 = (bf16[32,8,1664]{2,1,0:T(8,128)(2,1)}, bf16[32,8,1664]{2,1,0:T(8,128)(2,1)S(1)}, u32[]{:S(2)}) copy-start(bf16[32,8,1664]{2,1,0:T(8,128)(2,1)S(1)} %collective-permute-done) | copy-start | bytes 2555908

commit v2 on v1

v2 whole, which is shorter than its diff:
```python
import math

import jax
import jax.numpy as jnp
import numpy as np
from jax import lax
from jax.experimental import pallas as pl
from jax.experimental.pallas import tpu as pltpu
from jax.sharding import Mesh
from jax.sharding import PartitionSpec as P

N = 64
G_BLK = 1280
PAIRS = 256
ROWS = 160
MSG = 1664
F32 = jnp.float32
BF16 = jnp.bfloat16


def host_tables():
    k = np.arange(N)
    angle = 2.0 * math.pi * ((k[:, None] * k[None, :]) % N) / N
    c, s = np.cos(angle), np.sin(angle)
    top = np.concatenate([c, -s, -s, -c], axis=1)
    low = np.concatenate([s, c, c, -s], axis=1)
    z_table = np.concatenate([top, top, low, -low], axis=0)
    order = np.concatenate([k[0::2], k[1::2]])
    y_table = np.concatenate([c, s], axis=1)[order]
    to_re = np.stack([c, s], axis=1).reshape(2 * N, N)
    to_im = np.stack([-s, c], axis=1).reshape(2 * N, N)
    x_table = np.concatenate([to_re, to_im], axis=0)
    return z_table, y_table, x_table


def two_parts(table, axis):
    kind = np.dtype(BF16)
    high = table.astype(kind)
    return np.concatenate([high, (table - high.astype(np.float64)).astype(kind)], axis=axis)


def in_vmem(*arrays):
    return [pltpu.with_memory_space_constraint(a, pltpu.VMEM) for a in arrays]


def limit(mib):
    return pltpu.CompilerParams(vmem_limit_bytes=mib << 20)


SMEM = pl.BlockSpec(memory_space=pltpu.SMEM)
VMEM = pl.BlockSpec(memory_space=pltpu.VMEM)
ANY = pl.BlockSpec(memory_space=pl.ANY)


def local_dft_kernel(bands, val, cond, z_tab, y_tab, out, scratch):
    first = lax.broadcasted_iota(jnp.int32, (N // 2, 2 * N), 1) < N

    def along_z(i):
        v = val[bands[0, i]].astype(F32).reshape(8 * N, 2 * N)
        c = cond[bands[1, i]].astype(F32).reshape(8 * N, 2 * N)
        products = jnp.concatenate([v * c, v * pltpu.roll(c, N, 1)], axis=1).astype(BF16)
        both = jnp.dot(products, z_tab[...], preferred_element_type=F32)
        return both.astype(BF16)

    def along_y(i, mid):
        parts = []
        for x in range(8):
            rows = mid[x * N : (x + 1) * N]
            parts.append(jnp.concatenate([rows[:, : 2 * N], rows[:, 2 * N :]], axis=0))
        res = jnp.dot(y_tab[...], jnp.concatenate(parts, axis=1), preferred_element_type=F32)
        base = i * 8 * N
        for x in range(8):
            tile = res[:, x * 2 * N : (x + 1) * 2 * N]
            even, odd = tile[: N // 2], tile[N // 2 :]
            scratch[pl.ds(base + x * N, N // 2), :] = jnp.where(first, even, pltpu.roll(odd, N, 1))
            scratch[pl.ds(base + x * N + N // 2, N // 2), :] = jnp.where(first, pltpu.roll(even, N, 1), odd)

    def store(i):
        base = i * 8 * N
        for k in range(N // 2):
            rows = scratch[pl.ds(base + k, 16, stride=N // 2), :]
            out[k // 4, k % 4, pl.ds(16 * i, 16), :] = rows.astype(BF16)

    mids = [along_z(0)]
    for i in range(4):
        if i < 3:
            mids.append(along_z(i + 1))
        along_y(i, mids[i])
        store(i)


def local_dft(bands, psi_val, psi_cond, z_tab, y_tab):
    return pl.pallas_call(
        local_dft_kernel,
        in_specs=[SMEM, VMEM, VMEM, VMEM, VMEM],
        out_specs=VMEM,
        out_shape=pltpu.VMEM((8, 4, N, 2 * N), BF16),
        scratch_shapes=[pltpu.VMEM((4 * 8 * N, 2 * N), F32)],
        name="local_dft",
    )(bands, psi_val, psi_cond, z_tab, y_tab)


def picks_kernel(g_map, x_tab, column_pick, twiddle):
    g = g_map[...]
    row = lax.broadcasted_iota(jnp.int32, (8 * N, G_BLK), 0)
    column_pick[...] = jnp.where(row == (g & (8 * N - 1)), 1.0, 0.0).astype(BF16)
    row = lax.broadcasted_iota(jnp.int32, (2 * N, G_BLK), 0)
    x_pick = jnp.where((row & (N - 1)) == (g >> 12), 1.0, 0.0).astype(BF16)
    twiddle[...] = jnp.dot(x_tab[...], x_pick, preferred_element_type=F32)


def picks(g_map, x_tab):
    return pl.pallas_call(
        picks_kernel,
        in_specs=[VMEM, VMEM],
        out_specs=(VMEM, VMEM),
        out_shape=(pltpu.VMEM((8 * N, G_BLK), BF16), pltpu.VMEM((4 * N, G_BLK), F32)),
        compiler_params=limit(8),
        name="picks",
    )(g_map, x_tab)


def elements_kernel(bands, e_val, e_cond, slabs, column_pick, twiddle, elements, scaled):
    step = 256
    row = lax.broadcasted_iota(jnp.int32, (8, step), 0) % 4
    gap = jnp.zeros((8, step), F32)
    for i in range(4):
        gap = jnp.where(row == i, e_val[bands[0, i]] - e_cond[bands[1, i]], gap)
    weight = 2.0 / gap
    left = jnp.concatenate([slabs[:, s].reshape(8 * N, 2 * N) for s in range(4)], axis=1)
    for n in range(G_BLK // step):
        cols = pl.ds(n * step, step)
        picked = jnp.dot(left, column_pick[:, cols], preferred_element_type=F32)
        picked = picked.reshape(8, 4, 16, step)
        halves = []
        for h in range(2):
            factor = twiddle[pl.ds(h * 2 * N, 2 * N), cols].reshape(8, 1, 16, step)
            halves.append(jnp.sum(jnp.sum(picked * factor, axis=0), axis=1))
        values = (jnp.concatenate(halves, axis=0) * (1.0 / (N * 8))).astype(BF16)
        elements[:, cols] = values
        weighted = (weight * values.astype(F32)).astype(BF16)
        for f in range(8):
            scaled[f, :, cols] = weighted


def make_elements(bands, eps_val, eps_cond, slabs, column_pick, twiddle):
    return pl.pallas_call(
        elements_kernel,
        in_specs=[SMEM] * 3 + [VMEM] * 3,
        out_specs=(VMEM, VMEM),
        out_shape=(pltpu.VMEM((8, G_BLK), BF16), pltpu.VMEM((8, 8, G_BLK), BF16)),
        compiler_params=limit(12),
        name="elements",
    )(bands, eps_val, eps_cond, *in_vmem(slabs, column_pick, twiddle))


def messages_kernel(core, elements, scaled, out):
    swapped = core[0] == 1
    values = elements[...]
    pad = jnp.zeros((8, MSG - G_BLK - 2 * ROWS), F32)
    for j in range(32):
        out[j, :, pl.ds(0, G_BLK)] = values
        part = (j % 4) * 2 * ROWS
        rows = scaled[j // 4].astype(F32)[:, part : part + 2 * ROWS]
        first, second = rows[:, :ROWS], rows[:, ROWS:]
        mine = jnp.where(swapped, second, first)
        other = jnp.where(swapped, first, second)
        tail = jnp.concatenate([mine, pad, other], axis=1).astype(BF16)
        out[j, :, pl.ds(G_BLK, MSG - G_BLK)] = tail


def make_messages(core, elements, scaled):
    return pl.pallas_call(
        messages_kernel,
        in_specs=[SMEM, VMEM, VMEM],
        out_specs=VMEM,
        out_shape=pltpu.VMEM((32, 8, MSG), BF16),
        compiler_params=limit(4),
        name="messages",
    )(core, *in_vmem(elements, scaled))


def left_side(tail, skip):
    rows = tail.astype(F32)
    turned = pltpu.roll(rows.reshape(32, 8, 256), 4, 1)
    sign = jnp.where(lax.broadcasted_iota(jnp.int32, (32, 8, 256), 1) < 4, -1.0, 1.0)
    turned = (turned * sign).reshape(256, 256)
    keep = slice(skip, skip + ROWS)
    return jnp.concatenate([rows.T[keep].astype(BF16), turned.T[keep].astype(BF16)], axis=0)


def first_half_kernel(data, out):
    left = left_side(data[:, pl.ds(G_BLK, 256)], 0)
    for n in range(5):
        cols = pl.ds(n * 256, 256)
        out[:, cols] = jnp.dot(left, data[:, cols], preferred_element_type=F32)


def first_half(data):
    return pl.pallas_call(
        first_half_kernel,
        in_specs=[VMEM],
        out_specs=VMEM,
        out_shape=pltpu.VMEM((2 * ROWS, G_BLK), F32),
        compiler_params=limit(8),
        name="first_half",
    )(*in_vmem(data.reshape(256, MSG)))


def second_half_kernel(data, start, out, stage, sems):
    left = left_side(data[:, pl.ds(G_BLK + 128, 256)], 96)
    copies = []
    for n in range(5):
        cols = pl.ds(n * 256, 256)
        total = start[:, cols] + jnp.dot(left, data[:, cols], preferred_element_type=F32)
        total = total * (1.0 / PAIRS)
        stage[0, :, cols] = total[:ROWS]
        stage[1, :, cols] = total[ROWS:]
        copy = pltpu.make_async_copy(stage.at[:, :, cols], out.at[:, :, cols], sems.at[n])
        copy.start()
        copies.append(copy)
    for copy in copies:
        copy.wait()


def second_half(data, start):
    return pl.pallas_call(
        second_half_kernel,
        in_specs=[VMEM, VMEM],
        out_specs=ANY,
        out_shape=jax.ShapeDtypeStruct((2, ROWS, G_BLK), F32),
        scratch_shapes=[pltpu.VMEM((2, ROWS, G_BLK), F32), pltpu.SemaphoreType.DMA((5,))],
        compiler_params=limit(8),
        name="second_half",
    )(*in_vmem(data.reshape(256, MSG), start))


def on_device(psi_val, psi_cond, pair_bands, eps_val, eps_cond, g_map):
    z_table, y_table, x_table = host_tables()
    z_tab = jnp.asarray(z_table.astype(np.dtype(BF16)))
    y_tab = jnp.asarray(y_table.astype(np.dtype(BF16)))
    x_tab = jnp.asarray(two_parts(x_table, 1))
    bands = pair_bands.T
    slabs = local_dft(bands, psi_val, psi_cond, z_tab, y_tab)
    slabs = lax.all_to_all(slabs, ("x", "zl"), 0, 0, tiled=True)
    column_pick, twiddle = picks(g_map.reshape(1, G_BLK), x_tab)
    elements, scaled = make_elements(bands, eps_val, eps_cond, slabs, column_pick, twiddle)
    scaled = lax.all_to_all(scaled, ("x", "zl"), 0, 0, tiled=True)
    core = lax.axis_index("core").astype(jnp.int32).reshape(1)
    data = make_messages(core, elements, scaled)
    mine = lax.all_to_all(data, ("zh", "y"), 0, 0, tiled=True)
    other = lax.ppermute(mine, "core", [(0, 1), (1, 0)])
    return second_half(other, first_half(mine))


def solution(mesh):
    fine = Mesh(mesh.devices.reshape(4, 8, 2, 4, 2), ("zh", "y", "core", "x", "zl"))
    pair, fft = ("zh", "y", "core"), ("x", "zl")
    in_specs = (
        P(pair, fft, None, None),
        P(pair, fft, None, None),
        P(pair, None),
        P(pair),
        P(pair),
        P(fft),
    )
    return jax.shard_map(
        on_device, mesh=fine, in_specs=in_specs, out_specs=P(None, pair, fft), check_vma=False
    )
```

time: 92.5 us -> 79.3 us (0.86)
  Pallas kernels: 19.7 us -> 9.31 us
  local copies, waits for them, and re-layouts: 5.1 us -> 0.02 us
  waiting for transfers between devices: 12.7 us -> 15.5 us
    pallas_call x5 -> x6, Pallas kernels: 19.7 us -> 9.31 us  [the longest x1 3.72 us: local_dft(): pl.pallas_call(local_dft_kernel, in_specs=[SMEM, VMEM, VMEM, VMEM, VMEM],...]
    unnamed x11 -> x10, local copies, waits for them, and re-layouts: 3.06 us -> 0.02 us
    all_to_all x1, waiting for transfers between devices: 5.87 us -> 8.37 us  [on_device(): slabs = lax.all_to_all(slabs, ('x', 'zl'), 0, 0, tiled=True)]
    slice x2 -> x0, local copies, waits for them, and re-layouts: 1.45 us -> none  [product(): rows_m, rows_o = (mine[:, G_BLK:], other[:, G_BLK:])]
  transfers between devices with their start and end apart: 3 -> 3, of which waited for: 3 -> 3; matrix products, arithmetic and copies ran while one was open for 1% -> 0% of each run, Pallas kernels for 3% -> 2%
where the time goes in v2:
time: 79.3 us; the launch traced here: 78.9 us
  blocking collectives  38 us (48%)
  starting transfers between devices  16 us (20%)
  waiting for transfers between devices  15.5 us (20%)
  Pallas kernels  9.31 us (12%)
    all_to_all x1, blocking collectives, on_device(): mine = lax.all_to_all(data, ('zh', 'y'), 0, 0, tiled=True)  38 us
    all_to_all x1, waiting for transfers between devices, on_device(): slabs = lax.all_to_all(slabs, ('x', 'zl'), 0, 0, tiled=True)  8.37 us
    ppermute x1, starting transfers between devices, on_device(): other = lax.ppermute(mine, 'core', [(0, 1), (1, 0)])  6.76 us
    all_to_all x1, starting transfers between devices, on_device(): slabs = lax.all_to_all(slabs, ('x', 'zl'), 0, 0, tiled=True)  5.83 us
    all_to_all x1, waiting for transfers between devices, on_device(): scaled = lax.all_to_all(scaled, ('x', 'zl'), 0, 0, tiled=True)  5.6 us
    pallas_call x1, Pallas kernels, local_dft(): pl.pallas_call(local_dft_kernel, in_specs=[SMEM, VMEM, VMEM, VMEM, VMEM],...  3.72 us
    all_to_all x1, starting transfers between devices, on_device(): scaled = lax.all_to_all(scaled, ('x', 'zl'), 0, 0, tiled=True)  3.38 us
    pallas_call x1, Pallas kernels, make_elements(): pl.pallas_call(elements_kernel, in_specs=[SMEM] * 3 + [VMEM] * 3, out_spe...  2.15 us
  transfers between devices with their start and end apart: 3, of which 3 were waited for; matrix products, arithmetic and copies ran while one was open for 0% of the time, Pallas kernels for 2%

profile of v2, /device:TPU:9, one launch (start us, length us, event | category | flops | bytes accessed | tf_op | source)
XLA Modules:
  0.0 78.9 jit_solution(1190782853559401731)
XLA Ops:
  0.0 0.0 copy-start.4
  0.0 0.0 copy-start
  0.0 0.0 copy-start.1
  0.0 0.0 copy-start.2
  0.0 0.0 copy-start.3
  0.0 3.7 %local_dft.1 = bf16[8,4,64,128]{3,2,1,0:T(8,128)(2,1)} custom-call(s32[2,4]{1,0:T(2,128)} %bitcast.6, bf16[6,8,64,128]{3,2,1,0:T(8,128)(2,1)} %val.1, bf16[6,8,64,128]{3,2,1,0:T(8,128)(2,1)} %cond.1, bf16[256,256]{1,0:T(8,128)(2,1)} %constant.12.clone.z_tab, bf16[64,128]{1,0:T(8,128)(2,1)} %constant.13.clone.y_tab), custom_call_target="tpu_custom_call" | custom-call | tf_op jit(solution)/shard_map/local_dft/pallas_call | solution.py:93
  3.7 5.8 %all-to-all-start = ((bf16[8,4,64,128]{3,2,1,0:T(8,128)(2,1)}), bf16[8,4,64,128]{3,2,1,0:T(8,128)(2,1)S(1)}, u32[]{:S(2)}, u32[]{:S(2)}) async-start(bf16[8,4,64,128]{3,2,1,0:T(8,128)(2,1)} %local_dft.1), calls=%async_computation | async-start | bytes 1048576 | tf_op jit(solution)/shard_map/all_to_all | solution.py:245
  9.6 0.0 copy-done.4
  9.6 0.0 copy-done
  9.6 0.8 %picks.1 = (bf16[512,1280]{1,0:T(8,128)(2,1)S(1)}, f32[256,1280]{1,0:T(8,128)S(1)}) custom-call(s32[1,1280]{1,0:T(1,128)S(1)} %reshape.13.g_map, bf16[256,128]{1,0:T(8,128)(2,1)S(1)} %copy-done), custom_call_target="tpu_custom_call" | custom-call | tf_op jit(solution)/shard_map/picks/pallas_call | solution.py:113
  10.4 8.4 %all-to-all-done.slabs = bf16[8,4,64,128]{3,2,1,0:T(8,128)(2,1)S(1)} async-done(((bf16[8,4,64,128]{3,2,1,0:T(8,128)(2,1)}), bf16[8,4,64,128]{3,2,1,0:T(8,128)(2,1)S(1)}, u32[]{:S(2)}, u32[]{:S(2)}) %all-to-all-start) | async-done | bytes 524320 | tf_op jit(solution)/shard_map/all_to_all | solution.py:245
  18.8 0.0 copy-done.1
  18.8 0.0 copy-done.2
  18.8 0.0 copy-done.3
  18.8 2.2 %elements.1 = (bf16[8,1280]{1,0:T(8,128)(2,1)S(1)}, bf16[8,8,1280]{2,1,0:T(8,128)(2,1)}) custom-call(s32[2,4]{1,0:T(2,128)S(1)} %bitcast.7, f32[6]{0:T(128)S(1)} %copy-done.2, f32[6]{0:T(128)S(1)} %copy-done.3, bf16[8,4,64,128]{3,2,1,0:T(8,128)(2,1)S(1)} %all-to-all-done.slabs, bf16[512,1280]{1,0:T(8,128)(2,1)S(1)} %get-tuple-element.9.column_pick, ...), custom_call_target="tpu_custom_call" | custom-call | tf_op jit(solution)/shard_map/elements/pallas_call | solution.py:147
  21.0 3.4 %all-to-all-start.1 = ((bf16[8,8,1280]{2,1,0:T(8,128)(2,1)}), bf16[8,8,1280]{2,1,0:T(8,128)(2,1)S(1)}, u32[]{:S(2)}, u32[]{:S(2)}) async-start(bf16[8,8,1280]{2,1,0:T(8,128)(2,1)} %get-tuple-element.12), calls=%async_computation.1 | async-start | bytes 327680 | tf_op jit(solution)/shard_map/all_to_all | solution.py:248
  24.4 5.6 %all-to-all-done.1.scaled = bf16[8,8,1280]{2,1,0:T(8,128)(2,1)S(1)} async-done(((bf16[8,8,1280]{2,1,0:T(8,128)(2,1)}), bf16[8,8,1280]{2,1,0:T(8,128)(2,1)S(1)}, u32[]{:S(2)}, u32[]{:S(2)}) %all-to-all-start.1) | async-done | bytes 163872 | tf_op jit(solution)/shard_map/all_to_all | solution.py:248
  30.0 0.7 messages.1
  30.7 38.0 %all_to_all.15 = bf16[32,8,1664]{2,1,0:T(8,128)(2,1)S(1)} all-to-all(bf16[32,8,1664]{2,1,0:T(8,128)(2,1)S(1)} %messages.1), channel_id=1, replica_groups=mesh['zh'=4,'y'=8,'core'=2,'x'=4,'zl'=2] {'zh','y'}, dimensions={0} | all-to-all | bytes 1703936 | tf_op jit(solution)/shard_map/all_to_all | solution.py:251
  68.7 6.8 %collective-permute-start = (bf16[32,8,1664]{2,1,0:T(8,128)(2,1)S(1)}, bf16[32,8,1664]{2,1,0:T(8,128)(2,1)S(1)}, u32[]{:S(2)}, u32[]{:S(2)}) collective-permute-start(bf16[32,8,1664]{2,1,0:T(8,128)(2,1)S(1)} %all_to_all.15), channel_id=1, source_target_pairs={{0,8},{8,0},{1,9},{9,1},{2,10},{10,2},{3,11},{11,3},{4,12},{12,4},... | collective-permute-start | bytes 2555912 | tf_op jit(solution)/shard_map/ppermute | solution.py:252
  75.5 0.4 first_half.1.start
  75.9 1.6 %collective-permute-done = bf16[32,8,1664]{2,1,0:T(8,128)(2,1)S(1)} collective-permute-done((bf16[32,8,1664]{2,1,0:T(8,128)(2,1)S(1)}, bf16[32,8,1664]{2,1,0:T(8,128)(2,1)S(1)}, u32[]{:S(2)}, u32[]{:S(2)}) %collective-permute-start) | collective-permute-done | bytes 852000 | tf_op jit(solution)/shard_map/ppermute | solution.py:252
  77.4 1.5 %second_half.1 = f32[2,160,1280]{2,1,0:T(8,128)} custom-call(bf16[256,1664]{1,0:T(8,128)(2,1)S(1)} %bitcast.5, f32[320,1280]{1,0:T(8,128)S(1)} %first_half.1.start), custom_call_target="tpu_custom_call" | custom-call | tf_op jit(solution)/shard_map/second_half/pallas_call | solution.py:227
  (1 shorter events, 0.0 us)
Async XLA Ops:
  0.0 9.6 %copy-start.4 = (s32[1280]{0:T(1024)S(1)}, s32[1280]{0:T(1024)}, u32[]{:S(2)}) copy-start(s32[1280]{0:T(1024)} %param.14) | copy-start | bytes 15364
  0.0 9.6 %copy-start = (bf16[256,128]{1,0:T(8,128)(2,1)S(1)}, bf16[256,128]{1,0:T(8,128)(2,1)}, u32[]{:S(2)}) copy-start(bf16[256,128]{1,0:T(8,128)(2,1)} %constant.14.clone.x_tab) | copy-start | bytes 196612
  0.0 18.8 %copy-start.1 = (s32[4,2]{0,1:T(2,128)S(1)}, s32[4,2]{0,1:T(2,128)}, u32[]{:S(2)}) copy-start(s32[4,2]{0,1:T(2,128)} %param.11) | copy-start | bytes 100
  0.0 18.8 %copy-start.2 = (f32[6]{0:T(128)S(1)}, f32[6]{0:T(128)}, u32[]{:S(2)}) copy-start(f32[6]{0:T(128)} %e_val.1) | copy-start | bytes 76
  0.0 18.8 %copy-start.3 = (f32[6]{0:T(128)S(1)}, f32[6]{0:T(128)}, u32[]{:S(2)}) copy-start(f32[6]{0:T(128)} %e_cond.1) | copy-start | bytes 76
  3.7 15.1 %all-to-all-start = ((bf16[8,4,64,128]{3,2,1,0:T(8,128)(2,1)}), bf16[8,4,64,128]{3,2,1,0:T(8,128)(2,1)S(1)}, u32[]{:S(2)}, u32[]{:S(2)}) async-start(bf16[8,4,64,128]{3,2,1,0:T(8,128)(2,1)} %local_dft.1), calls=%async_computation | async-start | bytes 1048576 | tf_op jit(solution)/shard_map/all_to_all | solution.py:245
  21.0 9.0 %all-to-all-start.1 = ((bf16[8,8,1280]{2,1,0:T(8,128)(2,1)}), bf16[8,8,1280]{2,1,0:T(8,128)(2,1)S(1)}, u32[]{:S(2)}, u32[]{:S(2)}) async-start(bf16[8,8,1280]{2,1,0:T(8,128)(2,1)} %get-tuple-element.12), calls=%async_computation.1 | async-start | bytes 327680 | tf_op jit(solution)/shard_map/all_to_all | solution.py:248
  68.7 8.8 %collective-permute-start = (bf16[32,8,1664]{2,1,0:T(8,128)(2,1)S(1)}, bf16[32,8,1664]{2,1,0:T(8,128)(2,1)S(1)}, u32[]{:S(2)}, u32[]{:S(2)}) collective-permute-start(bf16[32,8,1664]{2,1,0:T(8,128)(2,1)S(1)} %all_to_all.15), channel_id=1, source_target_pairs={{0,8},{8,0},{1,9},{9,1},{2,10},{10,2},{3,11},{11,3},{4,12},{12,4},... | collective-permute-start | bytes 2555912 | tf_op jit(solution)/shard_map/ppermute | solution.py:252

commit v3 on v2

--- a/solution.py
+++ b/solution.py
@@ -56,9 +56,10 @@
     first = lax.broadcasted_iota(jnp.int32, (N // 2, 2 * N), 1) < N
 
     def along_z(i):
-        v = val[bands[0, i]].astype(F32).reshape(8 * N, 2 * N)
-        c = cond[bands[1, i]].astype(F32).reshape(8 * N, 2 * N)
-        products = jnp.concatenate([v * c, v * pltpu.roll(c, N, 1)], axis=1).astype(BF16)
+        v = val[bands[0, i]].reshape(8 * N, 2 * N)
+        c = cond[bands[1, i]].reshape(8 * N, 2 * N)
+        crossed = jnp.concatenate([c[:, N:], c[:, :N]], axis=1)
+        products = jnp.concatenate([v * c, v * crossed], axis=1)
         both = jnp.dot(products, z_tab[...], preferred_element_type=F32)
         return both.astype(BF16)
 
@@ -100,7 +101,12 @@
     )(bands, psi_val, psi_cond, z_tab, y_tab)
 
 
-def picks_kernel(g_map, x_tab, column_pick, twiddle):
+def picks_kernel(bands, e_val, e_cond, g_map, x_tab, column_pick, twiddle, weight):
+    row = lax.broadcasted_iota(jnp.int32, (8, 256), 0) % 4
+    gap = jnp.zeros((8, 256), F32)
+    for i in range(4):
+        gap = jnp.where(row == i, e_val[bands[0, i]] - e_cond[bands[1, i]], gap)
+    weight[...] = 2.0 / gap
     g = g_map[...]
     row = lax.broadcasted_iota(jnp.int32, (8 * N, G_BLK), 0)
     column_pick[...] = jnp.where(row == (g & (8 * N - 1)), 1.0, 0.0).astype(BF16)
@@ -109,24 +115,23 @@
     twiddle[...] = jnp.dot(x_tab[...], x_pick, preferred_element_type=F32)
 
 
-def picks(g_map, x_tab):
+def picks(bands, eps_val, eps_cond, g_map, x_tab):
     return pl.pallas_call(
         picks_kernel,
-        in_specs=[VMEM, VMEM],
-        out_specs=(VMEM, VMEM),
-        out_shape=(pltpu.VMEM((8 * N, G_BLK), BF16), pltpu.VMEM((4 * N, G_BLK), F32)),
+        in_specs=[SMEM] * 3 + [VMEM] * 2,
+        out_specs=(VMEM,) * 3,
+        out_shape=(
+            pltpu.VMEM((8 * N, G_BLK), BF16),
+            pltpu.VMEM((4 * N, G_BLK), F32),
+            pltpu.VMEM((8, 256), F32),
+        ),
         compiler_params=limit(8),
         name="picks",
-    )(g_map, x_tab)
-
-
-def elements_kernel(bands, e_val, e_cond, slabs, column_pick, twiddle, elements, scaled):
+    )(bands, eps_val, eps_cond, g_map, x_tab)
+
+
+def elements_kernel(slabs, column_pick, twiddle, weight, elements, scaled):
     step = 256
-    row = lax.broadcasted_iota(jnp.int32, (8, step), 0) % 4
-    gap = jnp.zeros((8, step), F32)
-    for i in range(4):
-        gap = jnp.where(row == i, e_val[bands[0, i]] - e_cond[bands[1, i]], gap)
-    weight = 2.0 / gap
     left = jnp.concatenate([slabs[:, s].reshape(8 * N, 2 * N) for s in range(4)], axis=1)
     for n in range(G_BLK // step):
         cols = pl.ds(n * step, step)
@@ -138,24 +143,24 @@
             halves.append(jnp.sum(jnp.sum(picked * factor, axis=0), axis=1))
         values = (jnp.concatenate(halves, axis=0) * (1.0 / (N * 8))).astype(BF16)
         elements[:, cols] = values
-        weighted = (weight * values.astype(F32)).astype(BF16)
+        weighted = (weight[...] * values.astype(F32)).astype(BF16)
         for f in range(8):
             scaled[f, :, cols] = weighted
 
 
-def make_elements(bands, eps_val, eps_cond, slabs, column_pick, twiddle):
+def make_elements(slabs, column_pick, twiddle, weight):
     return pl.pallas_call(
         elements_kernel,
-        in_specs=[SMEM] * 3 + [VMEM] * 3,
+        in_specs=[VMEM] * 4,
         out_specs=(VMEM, VMEM),
         out_shape=(pltpu.VMEM((8, G_BLK), BF16), pltpu.VMEM((8, 8, G_BLK), BF16)),
         compiler_params=limit(12),
         name="elements",
-    )(bands, eps_val, eps_cond, *in_vmem(slabs, column_pick, twiddle))
-
-
-def messages_kernel(core, elements, scaled, out):
-    swapped = core[0] == 1
+    )(*in_vmem(slabs, column_pick, twiddle, weight))
+
+
+def messages_kernel(elements, scaled, out):
+    swapped = lax.axis_index("core") == 1
     values = elements[...]
     pad = jnp.zeros((8, MSG - G_BLK - 2 * ROWS), F32)
     for j in range(32):
@@ -169,15 +174,15 @@
         out[j, :, pl.ds(G_BLK, MSG - G_BLK)] = tail
 
 
-def make_messages(core, elements, scaled):
+def make_messages(elements, scaled):
     return pl.pallas_call(
         messages_kernel,
-        in_specs=[SMEM, VMEM, VMEM],
+        in_specs=[VMEM, VMEM],
         out_specs=VMEM,
         out_shape=pltpu.VMEM((32, 8, MSG), BF16),
         compiler_params=limit(4),
         name="messages",
-    )(core, *in_vmem(elements, scaled))
+    )(*in_vmem(elements, scaled))
 
 
 def left_side(tail, skip):
@@ -243,11 +248,10 @@
     bands = pair_bands.T
     slabs = local_dft(bands, psi_val, psi_cond, z_tab, y_tab)
     slabs = lax.all_to_all(slabs, ("x", "zl"), 0, 0, tiled=True)
-    column_pick, twiddle = picks(g_map.reshape(1, G_BLK), x_tab)
-    elements, scaled = make_elements(bands, eps_val, eps_cond, slabs, column_pick, twiddle)
+    picked = picks(bands, eps_val, eps_cond, g_map.reshape(1, G_BLK), x_tab)
+    elements, scaled = make_elements(slabs, *picked)
     scaled = lax.all_to_all(scaled, ("x", "zl"), 0, 0, tiled=True)
-    core = lax.axis_index("core").astype(jnp.int32).reshape(1)
-    data = make_messages(core, elements, scaled)
+    data = make_messages(elements, scaled)
     mine = lax.all_to_all(data, ("zh", "y"), 0, 0, tiled=True)
     other = lax.ppermute(mine, "core", [(0, 1), (1, 0)])
     return second_half(other, first_half(mine))

time: 79.3 us -> 77.1 us (0.972)
  blocking collectives: 38 us -> 46.1 us
  waiting for transfers between devices: 15.5 us -> 9.35 us
  starting transfers between devices: 16 us -> 12.6 us
    all_to_all x0 -> x1, blocking collectives: none -> 8.07 us  [on_device(): scaled = lax.all_to_all(scaled, ('x', 'zl'), 0, 0, tiled=True)]
    all_to_all x1 -> x0, waiting for transfers between devices: 5.6 us -> none  [on_device(): scaled = lax.all_to_all(scaled, ('x', 'zl'), 0, 0, tiled=True)]
    all_to_all x1 -> x0, starting transfers between devices: 3.38 us -> none  [on_device(): scaled = lax.all_to_all(scaled, ('x', 'zl'), 0, 0, tiled=True)]
  transfers between devices with their start and end apart: 3 -> 2, of which waited for: 3 -> 2; matrix products, arithmetic and copies ran while one was open for 0% -> 0% of each run, Pallas kernels for 2% -> 2%
where the time goes in v3:
time: 77.1 us; the launch traced here: 76.8 us
  blocking collectives  46.1 us (60%)
  starting transfers between devices  12.6 us (16%)
  waiting for transfers between devices  9.35 us (12%)
  Pallas kernels  8.62 us (11%)
    all_to_all x1, blocking collectives, on_device(): mine = lax.all_to_all(data, ('zh', 'y'), 0, 0, tiled=True)  38.1 us
    all_to_all x1, blocking collectives, on_device(): scaled = lax.all_to_all(scaled, ('x', 'zl'), 0, 0, tiled=True)  8.07 us
    all_to_all x1, waiting for transfers between devices, on_device(): slabs = lax.all_to_all(slabs, ('x', 'zl'), 0, 0, tiled=True)  7.79 us
    ppermute x1, starting transfers between devices, on_device(): other = lax.ppermute(mine, 'core', [(0, 1), (1, 0)])  6.72 us
    all_to_all x1, starting transfers between devices, on_device(): slabs = lax.all_to_all(slabs, ('x', 'zl'), 0, 0, tiled=True)  5.83 us
    pallas_call x1, Pallas kernels, local_dft(): pl.pallas_call(local_dft_kernel, in_specs=[SMEM, VMEM, VMEM, VMEM, VMEM],...  3.7 us
    ppermute x1, waiting for transfers between devices, on_device(): other = lax.ppermute(mine, 'core', [(0, 1), (1, 0)])  1.55 us
  transfers between devices with their start and end apart: 2, of which 2 were waited for; matrix products, arithmetic and copies ran while one was open for 0% of the time, Pallas kernels for 2%

profile of v3, /device:TPU:9, one launch (start us, length us, event | category | flops | bytes accessed | tf_op | source)
XLA Modules:
  0.0 76.8 jit_solution(11689744135451375561)
XLA Ops:
  0.0 0.0 copy-start.4
  0.0 0.0 copy-start
  0.0 0.0 copy-start.1
  0.0 0.0 copy-start.2
  0.0 0.0 copy-start.3
  0.0 3.7 %local_dft.1 = bf16[8,4,64,128]{3,2,1,0:T(8,128)(2,1)} custom-call(s32[2,4]{1,0:T(2,128)} %bitcast.5, bf16[6,8,64,128]{3,2,1,0:T(8,128)(2,1)} %val.1, bf16[6,8,64,128]{3,2,1,0:T(8,128)(2,1)} %cond.1, bf16[256,256]{1,0:T(8,128)(2,1)} %constant.6.clone.z_tab, bf16[64,128]{1,0:T(8,128)(2,1)} %constant.7.clone.y_tab), custom_call_target="tpu_custom_call" | custom-call | tf_op jit(solution)/shard_map/local_dft/pallas_call | solution.py:94
  3.7 5.8 %all-to-all-start = ((bf16[8,4,64,128]{3,2,1,0:T(8,128)(2,1)}), bf16[8,4,64,128]{3,2,1,0:T(8,128)(2,1)S(1)}, u32[]{:S(2)}, u32[]{:S(2)}) async-start(bf16[8,4,64,128]{3,2,1,0:T(8,128)(2,1)} %local_dft.1), calls=%async_computation | async-start | bytes 1048576 | tf_op jit(solution)/shard_map/all_to_all | solution.py:250
  9.6 0.0 copy-done.4
  9.6 0.0 copy-done
  9.6 0.0 copy-done.1
  9.6 0.0 copy-done.2
  9.6 0.0 copy-done.3
  9.6 1.4 %picks.1 = (bf16[512,1280]{1,0:T(8,128)(2,1)S(1)}, f32[256,1280]{1,0:T(8,128)S(1)}, f32[8,256]{1,0:T(8,128)S(1)}) custom-call(s32[2,4]{1,0:T(2,128)S(1)} %bitcast.6, f32[6]{0:T(128)S(1)} %copy-done.2, f32[6]{0:T(128)S(1)} %copy-done.3, s32[1,1280]{1,0:T(1,128)S(1)} %reshape.9.g_map, bf16[256,128]{1,0:T(8,128)(2,1)S(1)} %copy-done), custom_call_target="tpu_custom_call" | custom-call | tf_op jit(solution)/shard_map/picks/pallas_call | solution.py:119
  11.0 7.8 %all-to-all-done.slabs = bf16[8,4,64,128]{3,2,1,0:T(8,128)(2,1)S(1)} async-done(((bf16[8,4,64,128]{3,2,1,0:T(8,128)(2,1)}), bf16[8,4,64,128]{3,2,1,0:T(8,128)(2,1)S(1)}, u32[]{:S(2)}, u32[]{:S(2)}) %all-to-all-start) | async-done | bytes 524320 | tf_op jit(solution)/shard_map/all_to_all | solution.py:250
  18.8 0.9 %elements.1 = (bf16[8,1280]{1,0:T(8,128)(2,1)S(1)}, bf16[8,8,1280]{2,1,0:T(8,128)(2,1)S(1)}) custom-call(bf16[8,4,64,128]{3,2,1,0:T(8,128)(2,1)S(1)} %all-to-all-done.slabs, bf16[512,1280]{1,0:T(8,128)(2,1)S(1)} %get-tuple-element.10.column_pick, f32[256,1280]{1,0:T(8,128)S(1)} %get-tuple-element.11.twiddle, f32[8,256]{1,0:T(8,128)S(1)} %get-tuple-element.12.weight), custom_call_target="tpu_custom_call" | custom-call | tf_op jit(solution)/shard_map/elements/pallas_call | solution.py:152
  19.7 8.1 %all_to_all.15.scaled = bf16[8,8,1280]{2,1,0:T(8,128)(2,1)S(1)} all-to-all(bf16[8,8,1280]{2,1,0:T(8,128)(2,1)S(1)} %get-tuple-element.14), channel_id=1, replica_groups=mesh['zh'=4,'y'=8,'core'=2,'x'=4,'zl'=2] {'x','zl'}, dimensions={0} | all-to-all | bytes 327680 | tf_op jit(solution)/shard_map/all_to_all | solution.py:253
  27.8 0.7 messages.1
  28.5 38.1 %all_to_all.16 = bf16[32,8,1664]{2,1,0:T(8,128)(2,1)S(1)} all-to-all(bf16[32,8,1664]{2,1,0:T(8,128)(2,1)S(1)} %messages.1), channel_id=1, replica_groups=mesh['zh'=4,'y'=8,'core'=2,'x'=4,'zl'=2] {'zh','y'}, dimensions={0} | all-to-all | bytes 1703936 | tf_op jit(solution)/shard_map/all_to_all | solution.py:255
  66.6 6.7 %collective-permute-start = (bf16[32,8,1664]{2,1,0:T(8,128)(2,1)S(1)}, bf16[32,8,1664]{2,1,0:T(8,128)(2,1)S(1)}, u32[]{:S(2)}, u32[]{:S(2)}) collective-permute-start(bf16[32,8,1664]{2,1,0:T(8,128)(2,1)S(1)} %all_to_all.16), channel_id=1, source_target_pairs={{0,8},{8,0},{1,9},{9,1},{2,10},{10,2},{3,11},{11,3},{4,12},{12,4},... | collective-permute-start | bytes 2555912 | tf_op jit(solution)/shard_map/ppermute | solution.py:256
  73.3 0.4 first_half.1.start
  73.7 1.6 %collective-permute-done = bf16[32,8,1664]{2,1,0:T(8,128)(2,1)S(1)} collective-permute-done((bf16[32,8,1664]{2,1,0:T(8,128)(2,1)S(1)}, bf16[32,8,1664]{2,1,0:T(8,128)(2,1)S(1)}, u32[]{:S(2)}, u32[]{:S(2)}) %collective-permute-start) | collective-permute-done | bytes 852000 | tf_op jit(solution)/shard_map/ppermute | solution.py:256
  75.3 1.5 %second_half.1 = f32[2,160,1280]{2,1,0:T(8,128)} custom-call(bf16[256,1664]{1,0:T(8,128)(2,1)S(1)} %bitcast.4, f32[320,1280]{1,0:T(8,128)S(1)} %first_half.1.start), custom_call_target="tpu_custom_call" | custom-call | tf_op jit(solution)/shard_map/second_half/pallas_call | solution.py:232
  (1 shorter events, 0.0 us)
Async XLA Ops:
  0.0 9.6 %copy-start.4 = (s32[1280]{0:T(1024)S(1)}, s32[1280]{0:T(1024)}, u32[]{:S(2)}) copy-start(s32[1280]{0:T(1024)} %param.14) | copy-start | bytes 15364
  0.0 9.6 %copy-start = (bf16[256,128]{1,0:T(8,128)(2,1)S(1)}, bf16[256,128]{1,0:T(8,128)(2,1)}, u32[]{:S(2)}) copy-start(bf16[256,128]{1,0:T(8,128)(2,1)} %constant.8.clone.x_tab) | copy-start | bytes 196612
  0.0 9.6 %copy-start.1 = (s32[4,2]{0,1:T(2,128)S(1)}, s32[4,2]{0,1:T(2,128)}, u32[]{:S(2)}) copy-start(s32[4,2]{0,1:T(2,128)} %param.11) | copy-start | bytes 100
  0.0 9.6 %copy-start.2 = (f32[6]{0:T(128)S(1)}, f32[6]{0:T(128)}, u32[]{:S(2)}) copy-start(f32[6]{0:T(128)} %e_val.1) | copy-start | bytes 76
  0.0 9.6 %copy-start.3 = (f32[6]{0:T(128)S(1)}, f32[6]{0:T(128)}, u32[]{:S(2)}) copy-start(f32[6]{0:T(128)} %e_cond.1) | copy-start | bytes 76
  3.7 15.1 %all-to-all-start = ((bf16[8,4,64,128]{3,2,1,0:T(8,128)(2,1)}), bf16[8,4,64,128]{3,2,1,0:T(8,128)(2,1)S(1)}, u32[]{:S(2)}, u32[]{:S(2)}) async-start(bf16[8,4,64,128]{3,2,1,0:T(8,128)(2,1)} %local_dft.1), calls=%async_computation | async-start | bytes 1048576 | tf_op jit(solution)/shard_map/all_to_all | solution.py:250
  66.6 8.7 %collective-permute-start = (bf16[32,8,1664]{2,1,0:T(8,128)(2,1)S(1)}, bf16[32,8,1664]{2,1,0:T(8,128)(2,1)S(1)}, u32[]{:S(2)}, u32[]{:S(2)}) collective-permute-start(bf16[32,8,1664]{2,1,0:T(8,128)(2,1)S(1)} %all_to_all.16), channel_id=1, source_target_pairs={{0,8},{8,0},{1,9},{9,1},{2,10},{10,2},{3,11},{11,3},{4,12},{12,4},... | collective-permute-start | bytes 2555912 | tf_op jit(solution)/shard_map/ppermute | solution.py:256

commit v4 on v3

--- a/solution.py
+++ b/solution.py
@@ -9,11 +9,12 @@
 from jax.sharding import Mesh
 from jax.sharding import PartitionSpec as P
 
+
 N = 64
 G_BLK = 1280
 PAIRS = 256
 ROWS = 160
-MSG = 1664
+TAIL = 384
 F32 = jnp.float32
 BF16 = jnp.bfloat16
 
@@ -130,9 +131,10 @@
     )(bands, eps_val, eps_cond, g_map, x_tab)
 
 
-def elements_kernel(slabs, column_pick, twiddle, weight, elements, scaled):
+def elements_kernel(slabs, column_pick, twiddle, weight, columns, *row_parts):
     step = 256
     left = jnp.concatenate([slabs[:, s].reshape(8 * N, 2 * N) for s in range(4)], axis=1)
+    weighted = []
     for n in range(G_BLK // step):
         cols = pl.ds(n * step, step)
         picked = jnp.dot(left, column_pick[:, cols], preferred_element_type=F32)
@@ -142,47 +144,80 @@
             factor = twiddle[pl.ds(h * 2 * N, 2 * N), cols].reshape(8, 1, 16, step)
             halves.append(jnp.sum(jnp.sum(picked * factor, axis=0), axis=1))
         values = (jnp.concatenate(halves, axis=0) * (1.0 / (N * 8))).astype(BF16)
-        elements[:, cols] = values
-        weighted = (weight[...] * values.astype(F32)).astype(BF16)
-        for f in range(8):
-            scaled[f, :, cols] = weighted
+        for j in range(32):
+            columns[j, :, cols] = values
+        weighted.append(weight[...] * values.astype(F32))
+    weighted = jnp.concatenate(weighted, axis=1)
+    swapped = lax.axis_index("core") == 1
+    index = lax.axis_index("y") & 3
+    pad = jnp.zeros((8, TAIL - 2 * ROWS), F32)
+    tails = []
+    for j in range(4):
+        rows = weighted[:, j * 2 * ROWS : (j + 1) * 2 * ROWS]
+        first, second = rows[:, :ROWS], rows[:, ROWS:]
+        mine = jnp.where(swapped, second, first)
+        other = jnp.where(swapped, first, second)
+        tails.append(jnp.concatenate([mine, pad, other], axis=1))
+    for s in range(4):
+        part = tails[s]
+        for i in range(1, 4):
+            part = jnp.where(index == i, tails[(i + s) % 4], part)
+        row_parts[s][...] = part.astype(BF16)
 
 
 def make_elements(slabs, column_pick, twiddle, weight):
     return pl.pallas_call(
         elements_kernel,
         in_specs=[VMEM] * 4,
-        out_specs=(VMEM, VMEM),
-        out_shape=(pltpu.VMEM((8, G_BLK), BF16), pltpu.VMEM((8, 8, G_BLK), BF16)),
+        out_specs=(VMEM,) * 5,
+        out_shape=(jax.ShapeDtypeStruct((32, 8, G_BLK), BF16),) + (pltpu.VMEM((8, TAIL), BF16),) * 4,
         compiler_params=limit(12),
         name="elements",
     )(*in_vmem(slabs, column_pick, twiddle, weight))
 
 
-def messages_kernel(elements, scaled, out):
+def pack_kernel(*refs):
+    parts, out = [r[...].astype(F32) for r in refs[:4]], refs[4]
+    index = lax.axis_index("y") & 3
+    for i in range(4):
+        part = parts[(0 - i) % 4]
+        for j in range(1, 4):
+            part = jnp.where(index == j, parts[(j - i) % 4], part)
+        out[i] = part.astype(BF16)
+
+
+def pack(parts):
+    return pl.pallas_call(
+        pack_kernel,
+        in_specs=[VMEM] * 4,
+        out_specs=VMEM,
+        out_shape=pltpu.VMEM((4, 8, TAIL), BF16),
+        compiler_params=limit(2),
+        name="pack",
+    )(*in_vmem(*parts))
+
+
+def spread_kernel(both, out):
     swapped = lax.axis_index("core") == 1
-    values = elements[...]
-    pad = jnp.zeros((8, MSG - G_BLK - 2 * ROWS), F32)
-    for j in range(32):
-        out[j, :, pl.ds(0, G_BLK)] = values
-        part = (j % 4) * 2 * ROWS
-        rows = scaled[j // 4].astype(F32)[:, part : part + 2 * ROWS]
-        first, second = rows[:, :ROWS], rows[:, ROWS:]
+    near = lax.broadcasted_iota(jnp.int32, (8, TAIL), 1) < TAIL // 2
+    for i in range(4):
+        first, second = both[0, i].astype(F32), both[1, i].astype(F32)
         mine = jnp.where(swapped, second, first)
         other = jnp.where(swapped, first, second)
-        tail = jnp.concatenate([mine, pad, other], axis=1).astype(BF16)
-        out[j, :, pl.ds(G_BLK, MSG - G_BLK)] = tail
-
-
-def make_messages(elements, scaled):
-    return pl.pallas_call(
-        messages_kernel,
-        in_specs=[VMEM, VMEM],
+        rows = jnp.where(near, mine, other).astype(BF16)
+        for f in range(8):
+            out[f, i] = rows
+
+
+def spread(both):
+    return pl.pallas_call(
+        spread_kernel,
+        in_specs=[VMEM],
         out_specs=VMEM,
-        out_shape=pltpu.VMEM((32, 8, MSG), BF16),
-        compiler_params=limit(4),
-        name="messages",
-    )(*in_vmem(elements, scaled))
+        out_shape=pltpu.VMEM((8, 4, 8, TAIL), BF16),
+        compiler_params=limit(2),
+        name="spread",
+    )(*in_vmem(both))
 
 
 def left_side(tail, skip):
@@ -194,30 +229,14 @@
     return jnp.concatenate([rows.T[keep].astype(BF16), turned.T[keep].astype(BF16)], axis=0)
 
 
-def first_half_kernel(data, out):
-    left = left_side(data[:, pl.ds(G_BLK, 256)], 0)
-    for n in range(5):
-        cols = pl.ds(n * 256, 256)
-        out[:, cols] = jnp.dot(left, data[:, cols], preferred_element_type=F32)
-
-
-def first_half(data):
-    return pl.pallas_call(
-        first_half_kernel,
-        in_specs=[VMEM],
-        out_specs=VMEM,
-        out_shape=pltpu.VMEM((2 * ROWS, G_BLK), F32),
-        compiler_params=limit(8),
-        name="first_half",
-    )(*in_vmem(data.reshape(256, MSG)))
-
-
-def second_half_kernel(data, start, out, stage, sems):
-    left = left_side(data[:, pl.ds(G_BLK + 128, 256)], 96)
+def product_kernel(rows, mine, other, out, stage, sems):
+    left_mine = left_side(rows[:, pl.ds(0, 256)], 0)
+    left_other = left_side(rows[:, pl.ds(128, 256)], 96)
     copies = []
     for n in range(5):
         cols = pl.ds(n * 256, 256)
-        total = start[:, cols] + jnp.dot(left, data[:, cols], preferred_element_type=F32)
+        total = jnp.dot(left_mine, mine[:, cols], preferred_element_type=F32)
+        total += jnp.dot(left_other, other[:, cols], preferred_element_type=F32)
         total = total * (1.0 / PAIRS)
         stage[0, :, cols] = total[:ROWS]
         stage[1, :, cols] = total[ROWS:]
@@ -228,16 +247,28 @@
         copy.wait()
 
 
-def second_half(data, start):
-    return pl.pallas_call(
-        second_half_kernel,
-        in_specs=[VMEM, VMEM],
+def product(rows, mine, other):
+    return pl.pallas_call(
+        product_kernel,
+        in_specs=[VMEM] * 3,
         out_specs=ANY,
         out_shape=jax.ShapeDtypeStruct((2, ROWS, G_BLK), F32),
         scratch_shapes=[pltpu.VMEM((2, ROWS, G_BLK), F32), pltpu.SemaphoreType.DMA((5,))],
         compiler_params=limit(8),
-        name="second_half",
-    )(*in_vmem(data.reshape(256, MSG), start))
+        name="product",
+    )(*in_vmem(rows.reshape(256, TAIL), mine.reshape(256, G_BLK), other.reshape(256, G_BLK)))
+
+
+AXES = ("zh", "y", "core", "x", "zl")
+
+
+def to_row_owner(part, shift):
+    sizes = (4, 8, 2, 4, 2)
+    pairs = []
+    for source, (zh, y, core, x, zl) in enumerate(np.ndindex(*sizes)):
+        target = (x, 4 * zl + (y + shift) % 4, core, zh, y // 4)
+        pairs.append((source, int(np.ravel_multi_index(target, sizes))))
+    return lax.ppermute(part, AXES, pairs)
 
 
 def on_device(psi_val, psi_cond, pair_bands, eps_val, eps_cond, g_map):
@@ -249,16 +280,19 @@
     slabs = local_dft(bands, psi_val, psi_cond, z_tab, y_tab)
     slabs = lax.all_to_all(slabs, ("x", "zl"), 0, 0, tiled=True)
     picked = picks(bands, eps_val, eps_cond, g_map.reshape(1, G_BLK), x_tab)
-    elements, scaled = make_elements(slabs, *picked)
-    scaled = lax.all_to_all(scaled, ("x", "zl"), 0, 0, tiled=True)
-    data = make_messages(elements, scaled)
-    mine = lax.all_to_all(data, ("zh", "y"), 0, 0, tiled=True)
+    columns, *row_parts = make_elements(slabs, *picked)
+    mine = lax.all_to_all(columns, ("zh", "y"), 0, 0, tiled=True)
+    parts = [to_row_owner(part, s) for s, part in enumerate(row_parts)]
+    packed = pack(parts)
+    both = lax.all_gather(packed[None], "core", axis=0, tiled=True)
+    rows = spread(both)
+    rows = lax.all_to_all(rows, ("x", "zl"), 0, 0, tiled=True)
     other = lax.ppermute(mine, "core", [(0, 1), (1, 0)])
-    return second_half(other, first_half(mine))
+    return product(rows, mine, other)
 
 
 def solution(mesh):
-    fine = Mesh(mesh.devices.reshape(4, 8, 2, 4, 2), ("zh", "y", "core", "x", "zl"))
+    fine = Mesh(mesh.devices.reshape(4, 8, 2, 4, 2), AXES)
     pair, fft = ("zh", "y", "core"), ("x", "zl")
     in_specs = (
         P(pair, fft, None, None),

time: 77.1 us -> 109 us (1.41)
  the two profiles are of different devices: /device:TPU:9 before, /device:TPU:1 now
where the time goes in v4:
time: 109 us
  blocking collectives  69 us (63%)
  starting transfers between devices  24.7 us (23%)
  Pallas kernels  7.79 us (7%)
  waiting for transfers between devices  7.43 us (7%)
    all_to_all x1, blocking collectives, on_device(): mine = lax.all_to_all(columns, ('zh', 'y'), 0, 0, tiled=True)  33.9 us
    all_to_all x1, blocking collectives, on_device(): rows = lax.all_to_all(rows, ('x', 'zl'), 0, 0, tiled=True)  31.9 us
    ppermute x4, starting transfers between devices, to_row_owner(): return lax.ppermute(part, AXES, pairs)  11.5 us
    all_to_all x1, starting transfers between devices, on_device(): slabs = lax.all_to_all(slabs, ('x', 'zl'), 0, 0, tiled=True)  6.65 us
    ppermute x1, starting transfers between devices, on_device(): other = lax.ppermute(mine, 'core', [(0, 1), (1, 0)])  6.53 us
    all_to_all x1, waiting for transfers between devices, on_device(): slabs = lax.all_to_all(slabs, ('x', 'zl'), 0, 0, tiled=True)  6.1 us
    pallas_call x1, Pallas kernels, local_dft(): pl.pallas_call(local_dft_kernel, in_specs=[SMEM, VMEM, VMEM, VMEM, VMEM],...  3.7 us
    all_gather x1, blocking collectives, on_device(): both = lax.all_gather(packed[None], 'core', axis=0, tiled=True)  3.22 us
  transfers between devices with their start and end apart: 6, of which 2 were waited for; matrix products, arithmetic and copies ran while one was open for 0% of the time, Pallas kernels for 1%

profile of v4, /device:TPU:1, one launch (start us, length us, event | category | flops | bytes accessed | tf_op | source)
XLA Modules:
  0.0 109.1 jit_solution(4936884121537212417)
XLA Ops:
  0.0 0.0 copy-start.4
  0.0 0.0 copy-start
  0.0 0.0 copy-start.1
  0.0 0.0 copy-start.2
  0.0 0.0 copy-start.3
  0.0 3.7 %local_dft.1 = bf16[8,4,64,128]{3,2,1,0:T(8,128)(2,1)} custom-call(s32[2,4]{1,0:T(2,128)} %bitcast.9, bf16[6,8,64,128]{3,2,1,0:T(8,128)(2,1)} %val.1, bf16[6,8,64,128]{3,2,1,0:T(8,128)(2,1)} %cond.1, bf16[256,256]{1,0:T(8,128)(2,1)} %constant.6.clone.z_tab, bf16[64,128]{1,0:T(8,128)(2,1)} %constant.7.clone.y_tab), custom_call_target="tpu_custom_call" | custom-call | tf_op jit(solution)/shard_map/local_dft/pallas_call | solution.py:95
  3.7 6.6 %all-to-all-start = ((bf16[8,4,64,128]{3,2,1,0:T(8,128)(2,1)}), bf16[8,4,64,128]{3,2,1,0:T(8,128)(2,1)S(1)}, u32[]{:S(2)}, u32[]{:S(2)}) async-start(bf16[8,4,64,128]{3,2,1,0:T(8,128)(2,1)} %local_dft.1), calls=%async_computation | async-start | bytes 1048576 | tf_op jit(solution)/shard_map/all_to_all | solution.py:281
  10.4 0.0 copy-done.4
  10.4 0.0 copy-done
  10.4 0.0 copy-done.1
  10.4 0.0 copy-done.2
  10.4 0.0 copy-done.3
  10.4 1.4 %picks.1 = (bf16[512,1280]{1,0:T(8,128)(2,1)S(1)}, f32[256,1280]{1,0:T(8,128)S(1)}, f32[8,256]{1,0:T(8,128)S(1)}) custom-call(s32[2,4]{1,0:T(2,128)S(1)} %bitcast.10, f32[6]{0:T(128)S(1)} %copy-done.2, f32[6]{0:T(128)S(1)} %copy-done.3, s32[1,1280]{1,0:T(1,128)S(1)} %reshape.12.g_map, bf16[256,128]{1,0:T(8,128)(2,1)S(1)} %copy-done), custom_call_target="tpu_custom_call" | custom-call | tf_op jit(solution)/shard_map/picks/pallas_call | solution.py:120
  11.8 6.1 %all-to-all-done.slabs = bf16[8,4,64,128]{3,2,1,0:T(8,128)(2,1)S(1)} async-done(((bf16[8,4,64,128]{3,2,1,0:T(8,128)(2,1)}), bf16[8,4,64,128]{3,2,1,0:T(8,128)(2,1)S(1)}, u32[]{:S(2)}, u32[]{:S(2)}) %all-to-all-start) | async-done | bytes 524320 | tf_op jit(solution)/shard_map/all_to_all | solution.py:281
  17.9 1.1 elements.1
  19.0 33.9 %all_to_all.15 = bf16[32,8,1280]{2,1,0:T(8,128)(2,1)S(1)} all-to-all(bf16[32,8,1280]{2,1,0:T(8,128)(2,1)S(1)} %get-tuple-element.20), channel_id=1, replica_groups=mesh['zh'=4,'y'=8,'core'=2,'x'=4,'zl'=2] {'zh','y'}, dimensions={0} | all-to-all | bytes 1310720 | tf_op jit(solution)/shard_map/all_to_all | solution.py:284
  52.9 6.5 %collective-permute-start.4 = (bf16[32,8,1280]{2,1,0:T(8,128)(2,1)S(1)}, bf16[32,8,1280]{2,1,0:T(8,128)(2,1)S(1)}, u32[]{:S(2)}, u32[]{:S(2)}) collective-permute-start(bf16[32,8,1280]{2,1,0:T(8,128)(2,1)S(1)} %all_to_all.15), channel_id=1, source_target_pairs={{0,8},{8,0},{1,9},{9,1},{2,10},{10,2},{3,11},{11,3},{4,12},{12,4},... | collective-permute-start | bytes 1966088 | tf_op jit(solution)/shard_map/ppermute | solution.py:290
  59.4 0.7 collective-permute-start
  60.1 5.0 %collective-permute-start.1 = (bf16[8,384]{1,0:T(8,128)(2,1)S(1)}, bf16[8,384]{1,0:T(8,128)(2,1)S(1)}, u32[]{:S(2)}, u32[]{:S(2)}) collective-permute-start(bf16[8,384]{1,0:T(8,128)(2,1)S(1)} %get-tuple-element.17), channel_id=1, source_target_pairs={{0,16},{1,80},{2,144},{3,208},{4,272},{5,336},{6,400},{7,464},{8,2... | collective-permute-start | bytes 18440 | tf_op jit(solution)/shard_map/ppermute | solution.py:271
  65.1 2.9 %collective-permute-start.2 = (bf16[8,384]{1,0:T(8,128)(2,1)S(1)}, bf16[8,384]{1,0:T(8,128)(2,1)S(1)}, u32[]{:S(2)}, u32[]{:S(2)}) collective-permute-start(bf16[8,384]{1,0:T(8,128)(2,1)S(1)} %get-tuple-element.18), channel_id=1, source_target_pairs={{0,32},{1,96},{2,160},{3,224},{4,288},{5,352},{6,416},{7,480},{8,4... | collective-permute-start | bytes 18440 | tf_op jit(solution)/shard_map/ppermute | solution.py:271
  68.0 3.0 %collective-permute-start.3 = (bf16[8,384]{1,0:T(8,128)(2,1)S(1)}, bf16[8,384]{1,0:T(8,128)(2,1)S(1)}, u32[]{:S(2)}, u32[]{:S(2)}) collective-permute-start(bf16[8,384]{1,0:T(8,128)(2,1)S(1)} %get-tuple-element.19), channel_id=1, source_target_pairs={{0,48},{1,112},{2,176},{3,240},{4,304},{5,368},{6,432},{7,496},{8,... | collective-permute-start | bytes 18440 | tf_op jit(solution)/shard_map/ppermute | solution.py:271
  71.0 0.0 collective-permute-done.refs_0_
  71.0 0.0 collective-permute-done.1.refs_1_
  71.0 0.0 collective-permute-done.2.refs_2_
  71.0 1.3 %collective-permute-done.3.refs_3_ = bf16[8,384]{1,0:T(8,128)(2,1)S(1)} collective-permute-done((bf16[8,384]{1,0:T(8,128)(2,1)S(1)}, bf16[8,384]{1,0:T(8,128)(2,1)S(1)}, u32[]{:S(2)}, u32[]{:S(2)}) %collective-permute-start.3) | collective-permute-done | bytes 6176 | tf_op jit(solution)/shard_map/ppermute | solution.py:271
  72.4 3.2 %all-gather = bf16[8,8,384]{2,1,0:T(8,128)(2,1)S(1)} all-gather(bf16[4,8,384]{2,1,0:T(8,128)(2,1)S(1)} %pack.1), channel_id=2, replica_groups=mesh['zh'=4,'y'=8,'core'=2,'x'=4,'zl'=2] {'core'}, dimensions={0}, use_global_device_ids=true | all-gather | bytes 73728 | tf_op jit(solution)/shard_map/all_gather | solution.py:287
  75.6 31.9 %all_to_all.16 = bf16[8,4,8,384]{3,2,1,0:T(8,128)(2,1)S(1)} all-to-all(bf16[8,4,8,384]{3,2,1,0:T(8,128)(2,1)S(1)} %spread.1), channel_id=1, replica_groups=mesh['zh'=4,'y'=8,'core'=2,'x'=4,'zl'=2] {'x','zl'}, dimensions={0} | all-to-all | bytes 393216 | tf_op jit(solution)/shard_map/all_to_all | solution.py:289
  107.5 0.0 collective-permute-done.4
  107.5 1.6 %product.1 = f32[2,160,1280]{2,1,0:T(8,128)} custom-call(bf16[256,384]{1,0:T(8,128)(2,1)S(1)} %bitcast.6, bf16[256,1280]{1,0:T(8,128)(2,1)S(1)} %bitcast.5, bf16[256,1280]{1,0:T(8,128)(2,1)S(1)} %bitcast.7), custom_call_target="tpu_custom_call" | custom-call | tf_op jit(solution)/shard_map/product/pallas_call | solution.py:251
  (3 shorter events, 0.0 us)
Async XLA Ops:
  0.0 10.4 %copy-start.4 = (s32[1280]{0:T(1024)S(1)}, s32[1280]{0:T(1024)}, u32[]{:S(2)}) copy-start(s32[1280]{0:T(1024)} %param.14) | copy-start | bytes 15364
  0.0 10.4 %copy-start = (bf16[256,128]{1,0:T(8,128)(2,1)S(1)}, bf16[256,128]{1,0:T(8,128)(2,1)}, u32[]{:S(2)}) copy-start(bf16[256,128]{1,0:T(8,128)(2,1)} %constant.8.clone.x_tab) | copy-start | bytes 196612
  0.0 10.4 %copy-start.1 = (s32[4,2]{0,1:T(2,128)S(1)}, s32[4,2]{0,1:T(2,128)}, u32[]{:S(2)}) copy-start(s32[4,2]{0,1:T(2,128)} %param.11) | copy-start | bytes 100
  0.0 10.4 %copy-start.2 = (f32[6]{0:T(128)S(1)}, f32[6]{0:T(128)}, u32[]{:S(2)}) copy-start(f32[6]{0:T(128)} %e_val.1) | copy-start | bytes 76
  0.0 10.4 %copy-start.3 = (f32[6]{0:T(128)S(1)}, f32[6]{0:T(128)}, u32[]{:S(2)}) copy-start(f32[6]{0:T(128)} %e_cond.1) | copy-start | bytes 76
  3.7 14.2 %all-to-all-start = ((bf16[8,4,64,128]{3,2,1,0:T(8,128)(2,1)}), bf16[8,4,64,128]{3,2,1,0:T(8,128)(2,1)S(1)}, u32[]{:S(2)}, u32[]{:S(2)}) async-start(bf16[8,4,64,128]{3,2,1,0:T(8,128)(2,1)} %local_dft.1), calls=%async_computation | async-start | bytes 1048576 | tf_op jit(solution)/shard_map/all_to_all | solution.py:281
  52.9 54.6 %collective-permute-start.4 = (bf16[32,8,1280]{2,1,0:T(8,128)(2,1)S(1)}, bf16[32,8,1280]{2,1,0:T(8,128)(2,1)S(1)}, u32[]{:S(2)}, u32[]{:S(2)}) collective-permute-start(bf16[32,8,1280]{2,1,0:T(8,128)(2,1)S(1)} %all_to_all.15), channel_id=1, source_target_pairs={{0,8},{8,0},{1,9},{9,1},{2,10},{10,2},{3,11},{11,3},{4,12},{12,4},... | collective-permute-start | bytes 1966088 | tf_op jit(solution)/shard_map/ppermute | solution.py:290
  59.4 11.6 %collective-permute-start = (bf16[8,384]{1,0:T(8,128)(2,1)S(1)}, bf16[8,384]{1,0:T(8,128)(2,1)S(1)}, u32[]{:S(2)}, u32[]{:S(2)}) collective-permute-start(bf16[8,384]{1,0:T(8,128)(2,1)S(1)} %get-tuple-element.16), channel_id=1, source_target_pairs={{0,0},{1,64},{2,128},{3,192},{4,256},{5,320},{6,384},{7,448},{8,8}... | collective-permute-start | bytes 18440 | tf_op jit(solution)/shard_map/ppermute | solution.py:271
  60.1 10.9 %collective-permute-start.1 = (bf16[8,384]{1,0:T(8,128)(2,1)S(1)}, bf16[8,384]{1,0:T(8,128)(2,1)S(1)}, u32[]{:S(2)}, u32[]{:S(2)}) collective-permute-start(bf16[8,384]{1,0:T(8,128)(2,1)S(1)} %get-tuple-element.17), channel_id=1, source_target_pairs={{0,16},{1,80},{2,144},{3,208},{4,272},{5,336},{6,400},{7,464},{8,2... | collective-permute-start | bytes 18440 | tf_op jit(solution)/shard_map/ppermute | solution.py:271
  65.1 5.9 %collective-permute-start.2 = (bf16[8,384]{1,0:T(8,128)(2,1)S(1)}, bf16[8,384]{1,0:T(8,128)(2,1)S(1)}, u32[]{:S(2)}, u32[]{:S(2)}) collective-permute-start(bf16[8,384]{1,0:T(8,128)(2,1)S(1)} %get-tuple-element.18), channel_id=1, source_target_pairs={{0,32},{1,96},{2,160},{3,224},{4,288},{5,352},{6,416},{7,480},{8,4... | collective-permute-start | bytes 18440 | tf_op jit(solution)/shard_map/ppermute | solution.py:271
  68.0 4.4 %collective-permute-start.3 = (bf16[8,384]{1,0:T(8,128)(2,1)S(1)}, bf16[8,384]{1,0:T(8,128)(2,1)S(1)}, u32[]{:S(2)}, u32[]{:S(2)}) collective-permute-start(bf16[8,384]{1,0:T(8,128)(2,1)S(1)} %get-tuple-element.19), channel_id=1, source_target_pairs={{0,48},{1,112},{2,176},{3,240},{4,304},{5,368},{6,432},{7,496},{8,... | collective-permute-start | bytes 18440 | tf_op jit(solution)/shard_map/ppermute | solution.py:271

commit v5 on v4

--- a/solution.py
+++ b/solution.py
@@ -131,7 +131,7 @@
     )(bands, eps_val, eps_cond, g_map, x_tab)
 
 
-def elements_kernel(slabs, column_pick, twiddle, weight, columns, *row_parts):
+def elements_kernel(slabs, column_pick, twiddle, weight, columns, row_parts):
     step = 256
     left = jnp.concatenate([slabs[:, s].reshape(8 * N, 2 * N) for s in range(4)], axis=1)
     weighted = []
@@ -149,52 +149,24 @@
         weighted.append(weight[...] * values.astype(F32))
     weighted = jnp.concatenate(weighted, axis=1)
     swapped = lax.axis_index("core") == 1
-    index = lax.axis_index("y") & 3
     pad = jnp.zeros((8, TAIL - 2 * ROWS), F32)
-    tails = []
     for j in range(4):
         rows = weighted[:, j * 2 * ROWS : (j + 1) * 2 * ROWS]
         first, second = rows[:, :ROWS], rows[:, ROWS:]
         mine = jnp.where(swapped, second, first)
         other = jnp.where(swapped, first, second)
-        tails.append(jnp.concatenate([mine, pad, other], axis=1))
-    for s in range(4):
-        part = tails[s]
-        for i in range(1, 4):
-            part = jnp.where(index == i, tails[(i + s) % 4], part)
-        row_parts[s][...] = part.astype(BF16)
+        row_parts[j] = jnp.concatenate([mine, pad, other], axis=1).astype(BF16)
 
 
 def make_elements(slabs, column_pick, twiddle, weight):
     return pl.pallas_call(
         elements_kernel,
         in_specs=[VMEM] * 4,
-        out_specs=(VMEM,) * 5,
-        out_shape=(jax.ShapeDtypeStruct((32, 8, G_BLK), BF16),) + (pltpu.VMEM((8, TAIL), BF16),) * 4,
+        out_specs=(VMEM, VMEM),
+        out_shape=(pltpu.VMEM((32, 8, G_BLK), BF16), pltpu.VMEM((4, 8, TAIL), BF16)),
         compiler_params=limit(12),
         name="elements",
     )(*in_vmem(slabs, column_pick, twiddle, weight))
-
-
-def pack_kernel(*refs):
-    parts, out = [r[...].astype(F32) for r in refs[:4]], refs[4]
-    index = lax.axis_index("y") & 3
-    for i in range(4):
-        part = parts[(0 - i) % 4]
-        for j in range(1, 4):
-            part = jnp.where(index == j, parts[(j - i) % 4], part)
-        out[i] = part.astype(BF16)
-
-
-def pack(parts):
-    return pl.pallas_call(
-        pack_kernel,
-        in_specs=[VMEM] * 4,
-        out_specs=VMEM,
-        out_shape=pltpu.VMEM((4, 8, TAIL), BF16),
-        compiler_params=limit(2),
-        name="pack",
-    )(*in_vmem(*parts))
 
 
 def spread_kernel(both, out):
@@ -230,8 +202,10 @@
 
 
 def product_kernel(rows, mine, other, out, stage, sems):
-    left_mine = left_side(rows[:, pl.ds(0, 256)], 0)
-    left_other = left_side(rows[:, pl.ds(128, 256)], 96)
+    order = [(zh ^ 2) * 2 + 1 - half for zh in range(4) for half in range(2)]
+    panel = jnp.concatenate([rows[pl.ds(32 * k, 32), :] for k in order], axis=0)
+    left_mine = left_side(panel[:, :256], 0)
+    left_other = left_side(panel[:, 128:], 96)
     copies = []
     for n in range(5):
         cols = pl.ds(n * 256, 256)
@@ -259,16 +233,16 @@
     )(*in_vmem(rows.reshape(256, TAIL), mine.reshape(256, G_BLK), other.reshape(256, G_BLK)))
 
 
-AXES = ("zh", "y", "core", "x", "zl")
-
-
-def to_row_owner(part, shift):
-    sizes = (4, 8, 2, 4, 2)
+AXES = ("zh", "yh", "yl", "core", "x", "zl")
+
+
+def to_row_owner(parts):
+    sizes = (4, 2, 4, 2, 4, 2)
     pairs = []
-    for source, (zh, y, core, x, zl) in enumerate(np.ndindex(*sizes)):
-        target = (x, 4 * zl + (y + shift) % 4, core, zh, y // 4)
+    for source, (zh, yh, yl, core, x, zl) in enumerate(np.ndindex(*sizes)):
+        target = (x, zl, yl, core, zh ^ 2, 1 - yh)
         pairs.append((source, int(np.ravel_multi_index(target, sizes))))
-    return lax.ppermute(part, AXES, pairs)
+    return lax.ppermute(parts, AXES, pairs)
 
 
 def on_device(psi_val, psi_cond, pair_bands, eps_val, eps_cond, g_map):
@@ -280,20 +254,19 @@
     slabs = local_dft(bands, psi_val, psi_cond, z_tab, y_tab)
     slabs = lax.all_to_all(slabs, ("x", "zl"), 0, 0, tiled=True)
     picked = picks(bands, eps_val, eps_cond, g_map.reshape(1, G_BLK), x_tab)
-    columns, *row_parts = make_elements(slabs, *picked)
-    mine = lax.all_to_all(columns, ("zh", "y"), 0, 0, tiled=True)
-    parts = [to_row_owner(part, s) for s, part in enumerate(row_parts)]
-    packed = pack(parts)
-    both = lax.all_gather(packed[None], "core", axis=0, tiled=True)
-    rows = spread(both)
-    rows = lax.all_to_all(rows, ("x", "zl"), 0, 0, tiled=True)
+    columns, row_parts = make_elements(slabs, *picked)
+    mine = lax.all_to_all(columns, ("zh", "yh", "yl"), 0, 0, tiled=True)
+    parts = to_row_owner(row_parts)
+    both = lax.all_gather(parts[None], "core", axis=0, tiled=True)
+    rows = spread(both).reshape(32, 8, TAIL)
+    rows = lax.all_to_all(rows, ("x", "zl", "yl"), 0, 0, tiled=True)
     other = lax.ppermute(mine, "core", [(0, 1), (1, 0)])
     return product(rows, mine, other)
 
 
 def solution(mesh):
-    fine = Mesh(mesh.devices.reshape(4, 8, 2, 4, 2), AXES)
-    pair, fft = ("zh", "y", "core"), ("x", "zl")
+    fine = Mesh(mesh.devices.reshape(4, 2, 4, 2, 4, 2), AXES)
+    pair, fft = ("zh", "yh", "yl", "core"), ("x", "zl")
     in_specs = (
         P(pair, fft, None, None),
         P(pair, fft, None, None),

time: 109 us -> 91.2 us (0.84)
  the two profiles are of different devices: /device:TPU:1 before, /device:TPU:8 now
where the time goes in v5:
time: 91.2 us; the launch traced here: 90.8 us
  blocking collectives  51.9 us (57%)
  waiting for transfers between devices  19.8 us (22%)
  starting transfers between devices  11.3 us (12%)
  Pallas kernels  7.74 us (8%)
    all_to_all x1, blocking collectives, on_device(): mine = lax.all_to_all(columns, ('zh', 'yh', 'yl'), 0, 0, tiled=True)  36.8 us
    all_to_all x1, blocking collectives, on_device(): rows = lax.all_to_all(rows, ('x', 'zl', 'yl'), 0, 0, tiled=True)  13.3 us
    ppermute x1, waiting for transfers between devices, to_row_owner(): return lax.ppermute(parts, AXES, pairs)  11.1 us
    all_to_all x1, waiting for transfers between devices, on_device(): slabs = lax.all_to_all(slabs, ('x', 'zl'), 0, 0, tiled=True)  8.64 us
    all_to_all x1, starting transfers between devices, on_device(): slabs = lax.all_to_all(slabs, ('x', 'zl'), 0, 0, tiled=True)  6.1 us
    pallas_call x1, Pallas kernels, local_dft(): pl.pallas_call(local_dft_kernel, in_specs=[SMEM, VMEM, VMEM, VMEM, VMEM],...  3.7 us
    ppermute x1, starting transfers between devices, to_row_owner(): return lax.ppermute(parts, AXES, pairs)  3.31 us
    ppermute x1, starting transfers between devices, on_device(): other = lax.ppermute(mine, 'core', [(0, 1), (1, 0)])  1.91 us
  transfers between devices with their start and end apart: 3, of which 2 were waited for; matrix products, arithmetic and copies ran while one was open for 0% of the time, Pallas kernels for 2%

profile of v5, /device:TPU:8, one launch (start us, length us, event | category | flops | bytes accessed | tf_op | source)
XLA Modules:
  0.0 90.8 jit_solution(18239059026553299623)
XLA Ops:
  0.0 0.0 copy-start.4
  0.0 0.0 copy-start
  0.0 0.0 copy-start.1
  0.0 0.0 copy-start.2
  0.0 0.0 copy-start.3
  0.0 3.7 %local_dft.1 = bf16[8,4,64,128]{3,2,1,0:T(8,128)(2,1)} custom-call(s32[2,4]{1,0:T(2,128)} %bitcast.11, bf16[6,8,64,128]{3,2,1,0:T(8,128)(2,1)} %val.1, bf16[6,8,64,128]{3,2,1,0:T(8,128)(2,1)} %cond.1, bf16[256,256]{1,0:T(8,128)(2,1)} %constant.6.clone.z_tab, bf16[64,128]{1,0:T(8,128)(2,1)} %constant.7.clone.y_tab), custom_call_target="tpu_custom_call" | custom-call | tf_op jit(solution)/shard_map/local_dft/pallas_call | solution.py:95
  3.7 6.1 %all-to-all-start = ((bf16[8,4,64,128]{3,2,1,0:T(8,128)(2,1)}), bf16[8,4,64,128]{3,2,1,0:T(8,128)(2,1)S(1)}, u32[]{:S(2)}, u32[]{:S(2)}) async-start(bf16[8,4,64,128]{3,2,1,0:T(8,128)(2,1)} %local_dft.1), calls=%async_computation | async-start | bytes 1048576 | tf_op jit(solution)/shard_map/all_to_all | solution.py:255
  9.8 0.0 copy-done.4
  9.9 0.0 copy-done
  9.9 0.0 copy-done.1
  9.9 0.0 copy-done.2
  9.9 0.0 copy-done.3
  9.9 1.4 %picks.1 = (bf16[512,1280]{1,0:T(8,128)(2,1)S(1)}, f32[256,1280]{1,0:T(8,128)S(1)}, f32[8,256]{1,0:T(8,128)S(1)}) custom-call(s32[2,4]{1,0:T(2,128)S(1)} %bitcast.12, f32[6]{0:T(128)S(1)} %copy-done.2, f32[6]{0:T(128)S(1)} %copy-done.3, s32[1,1280]{1,0:T(1,128)S(1)} %reshape.15.g_map, bf16[256,128]{1,0:T(8,128)(2,1)S(1)} %copy-done), custom_call_target="tpu_custom_call" | custom-call | tf_op jit(solution)/shard_map/picks/pallas_call | solution.py:120
  11.3 8.6 %all-to-all-done.slabs = bf16[8,4,64,128]{3,2,1,0:T(8,128)(2,1)S(1)} async-done(((bf16[8,4,64,128]{3,2,1,0:T(8,128)(2,1)}), bf16[8,4,64,128]{3,2,1,0:T(8,128)(2,1)S(1)}, u32[]{:S(2)}, u32[]{:S(2)}) %all-to-all-start) | async-done | bytes 524320 | tf_op jit(solution)/shard_map/all_to_all | solution.py:255
  19.9 1.1 %elements.1 = (bf16[32,8,1280]{2,1,0:T(8,128)(2,1)S(1)}, bf16[4,8,384]{2,1,0:T(8,128)(2,1)S(1)}) custom-call(bf16[8,4,64,128]{3,2,1,0:T(8,128)(2,1)S(1)} %all-to-all-done.slabs, bf16[512,1280]{1,0:T(8,128)(2,1)S(1)} %get-tuple-element.10.column_pick, f32[256,1280]{1,0:T(8,128)S(1)} %get-tuple-element.11.twiddle, f32[8,256]{1,0:T(8,128)S(1)} %get-tuple-element.12.weight), custom_call_target="tpu_custom_call" | custom-call | tf_op jit(solution)/shard_map/elements/pallas_call | solution.py:162
  21.0 36.8 %all_to_all.15 = bf16[32,8,1280]{2,1,0:T(8,128)(2,1)S(1)} all-to-all(bf16[32,8,1280]{2,1,0:T(8,128)(2,1)S(1)} %get-tuple-element.14), channel_id=1, replica_groups=mesh['zh'=4,'yh'=2,'yl'=4,'core'=2,'x'=4,'zl'=2] {'zh','yh','yl'}, dimensions={0} | all-to-all | bytes 1310720 | tf_op jit(solution)/shard_map/all_to_all | solution.py:258
  57.8 1.9 %collective-permute-start.1 = (bf16[32,8,1280]{2,1,0:T(8,128)(2,1)S(1)}, bf16[32,8,1280]{2,1,0:T(8,128)(2,1)S(1)}, u32[]{:S(2)}, u32[]{:S(2)}) collective-permute-start(bf16[32,8,1280]{2,1,0:T(8,128)(2,1)S(1)} %all_to_all.15), channel_id=1, source_target_pairs={{0,8},{8,0},{1,9},{9,1},{2,10},{10,2},{3,11},{11,3},{4,12},{12,4},... | collective-permute-start | bytes 1966088 | tf_op jit(solution)/shard_map/ppermute | solution.py:263
  59.7 3.3 %collective-permute-start = (bf16[4,8,384]{2,1,0:T(8,128)(2,1)S(1)}, bf16[4,8,384]{2,1,0:T(8,128)(2,1)S(1)}, u32[]{:S(2)}, u32[]{:S(2)}) collective-permute-start(bf16[4,8,384]{2,1,0:T(8,128)(2,1)S(1)} %get-tuple-element.13), channel_id=1, source_target_pairs={{0,5},{1,69},{2,133},{3,197},{4,261},{5,325},{6,389},{7,453},{8,13... | collective-permute-start | bytes 73736 | tf_op jit(solution)/shard_map/ppermute | solution.py:245
  63.0 11.1 %collective-permute-done = bf16[4,8,384]{2,1,0:T(8,128)(2,1)S(1)} collective-permute-done((bf16[4,8,384]{2,1,0:T(8,128)(2,1)S(1)}, bf16[4,8,384]{2,1,0:T(8,128)(2,1)S(1)}, u32[]{:S(2)}, u32[]{:S(2)}) %collective-permute-start) | collective-permute-done | bytes 24608 | tf_op jit(solution)/shard_map/ppermute | solution.py:245
  74.1 1.8 %all-gather = bf16[8,8,384]{2,1,0:T(8,128)(2,1)S(1)} all-gather(bf16[4,8,384]{2,1,0:T(8,128)(2,1)S(1)} %collective-permute-done), channel_id=2, replica_groups=mesh['zh'=4,'yh'=2,'yl'=4,'core'=2,'x'=4,'zl'=2] {'core'}, dimensions={0}, use_global_device_ids=true | all-gather | bytes 73728 | tf_op jit(solution)/shard_map/all_gather | solution.py:260
  76.0 13.3 %all_to_all.16 = bf16[32,8,384]{2,1,0:T(8,128)(2,1)S(1)} all-to-all(bf16[32,8,384]{2,1,0:T(8,128)(2,1)S(1)} %bitcast.8), channel_id=1, replica_groups=mesh['zh'=4,'yh'=2,'yl'=4,'core'=2,'x'=4,'zl'=2] {'x','zl','yl'}, dimensions={0} | all-to-all | bytes 393216 | tf_op jit(solution)/shard_map/all_to_all | solution.py:262
  89.3 0.0 collective-permute-done.1
  89.3 1.6 %product.1 = f32[2,160,1280]{2,1,0:T(8,128)} custom-call(bf16[256,384]{1,0:T(8,128)(2,1)S(1)} %bitcast.7, bf16[256,1280]{1,0:T(8,128)(2,1)S(1)} %bitcast.6, bf16[256,1280]{1,0:T(8,128)(2,1)S(1)} %bitcast.9), custom_call_target="tpu_custom_call" | custom-call | tf_op jit(solution)/shard_map/product/pallas_call | solution.py:225
  (2 shorter events, 0.0 us)
Async XLA Ops:
  0.0 9.8 %copy-start.4 = (s32[1280]{0:T(1024)S(1)}, s32[1280]{0:T(1024)}, u32[]{:S(2)}) copy-start(s32[1280]{0:T(1024)} %param.14) | copy-start | bytes 15364
  0.0 9.9 %copy-start = (bf16[256,128]{1,0:T(8,128)(2,1)S(1)}, bf16[256,128]{1,0:T(8,128)(2,1)}, u32[]{:S(2)}) copy-start(bf16[256,128]{1,0:T(8,128)(2,1)} %constant.8.clone.x_tab) | copy-start | bytes 196612
  0.0 9.9 %copy-start.1 = (s32[4,2]{0,1:T(2,128)S(1)}, s32[4,2]{0,1:T(2,128)}, u32[]{:S(2)}) copy-start(s32[4,2]{0,1:T(2,128)} %param.11) | copy-start | bytes 100
  0.0 9.9 %copy-start.2 = (f32[6]{0:T(128)S(1)}, f32[6]{0:T(128)}, u32[]{:S(2)}) copy-start(f32[6]{0:T(128)} %e_val.1) | copy-start | bytes 76
  0.0 9.9 %copy-start.3 = (f32[6]{0:T(128)S(1)}, f32[6]{0:T(128)}, u32[]{:S(2)}) copy-start(f32[6]{0:T(128)} %e_cond.1) | copy-start | bytes 76
  3.7 16.2 %all-to-all-start = ((bf16[8,4,64,128]{3,2,1,0:T(8,128)(2,1)}), bf16[8,4,64,128]{3,2,1,0:T(8,128)(2,1)S(1)}, u32[]{:S(2)}, u32[]{:S(2)}) async-start(bf16[8,4,64,128]{3,2,1,0:T(8,128)(2,1)} %local_dft.1), calls=%async_computation | async-start | bytes 1048576 | tf_op jit(solution)/shard_map/all_to_all | solution.py:255
  57.8 31.5 %collective-permute-start.1 = (bf16[32,8,1280]{2,1,0:T(8,128)(2,1)S(1)}, bf16[32,8,1280]{2,1,0:T(8,128)(2,1)S(1)}, u32[]{:S(2)}, u32[]{:S(2)}) collective-permute-start(bf16[32,8,1280]{2,1,0:T(8,128)(2,1)S(1)} %all_to_all.15), channel_id=1, source_target_pairs={{0,8},{8,0},{1,9},{9,1},{2,10},{10,2},{3,11},{11,3},{4,12},{12,4},... | collective-permute-start | bytes 1966088 | tf_op jit(solution)/shard_map/ppermute | solution.py:263
  59.7 14.4 %collective-permute-start = (bf16[4,8,384]{2,1,0:T(8,128)(2,1)S(1)}, bf16[4,8,384]{2,1,0:T(8,128)(2,1)S(1)}, u32[]{:S(2)}, u32[]{:S(2)}) collective-permute-start(bf16[4,8,384]{2,1,0:T(8,128)(2,1)S(1)} %get-tuple-element.13), channel_id=1, source_target_pairs={{0,5},{1,69},{2,133},{3,197},{4,261},{5,325},{6,389},{7,453},{8,13... | collective-permute-start | bytes 73736 | tf_op jit(solution)/shard_map/ppermute | solution.py:245

commit v6 on v3

--- a/solution.py
+++ b/solution.py
@@ -11,6 +11,7 @@
 
 N = 64
 G_BLK = 1280
+PITCH = 33
 PAIRS = 256
 ROWS = 160
 MSG = 1664
@@ -69,17 +70,18 @@
             rows = mid[x * N : (x + 1) * N]
             parts.append(jnp.concatenate([rows[:, : 2 * N], rows[:, 2 * N :]], axis=0))
         res = jnp.dot(y_tab[...], jnp.concatenate(parts, axis=1), preferred_element_type=F32)
-        base = i * 8 * N
+        base = i * 16 * PITCH
         for x in range(8):
             tile = res[:, x * 2 * N : (x + 1) * 2 * N]
             even, odd = tile[: N // 2], tile[N // 2 :]
-            scratch[pl.ds(base + x * N, N // 2), :] = jnp.where(first, even, pltpu.roll(odd, N, 1))
-            scratch[pl.ds(base + x * N + N // 2, N // 2), :] = jnp.where(first, pltpu.roll(even, N, 1), odd)
+            turned = pltpu.roll(jnp.where(first, odd, even), N, 1)
+            scratch[pl.ds(base + 2 * x * PITCH, N // 2), :] = jnp.where(first, even, turned)
+            scratch[pl.ds(base + (2 * x + 1) * PITCH, N // 2), :] = jnp.where(first, turned, odd)
 
     def store(i):
-        base = i * 8 * N
+        base = i * 16 * PITCH
         for k in range(N // 2):
-            rows = scratch[pl.ds(base + k, 16, stride=N // 2), :]
+            rows = scratch[pl.ds(base + k, 16, stride=PITCH), :]
             out[k // 4, k % 4, pl.ds(16 * i, 16), :] = rows.astype(BF16)
 
     mids = [along_z(0)]
@@ -96,7 +98,7 @@
         in_specs=[SMEM, VMEM, VMEM, VMEM, VMEM],
         out_specs=VMEM,
         out_shape=pltpu.VMEM((8, 4, N, 2 * N), BF16),
-        scratch_shapes=[pltpu.VMEM((4 * 8 * N, 2 * N), F32)],
+        scratch_shapes=[pltpu.VMEM((4 * 16 * PITCH, 2 * N), F32)],
         name="local_dft",
     )(bands, psi_val, psi_cond, z_tab, y_tab)
 

time: 77.1 us -> 76.6 us (level)
  no operation moved by 1% of the time
where the time goes in v6:
time: 76.6 us; the launch traced here: 76.3 us
  blocking collectives  46.1 us (60%)
  starting transfers between devices  12.6 us (16%)
  waiting for transfers between devices  9.35 us (12%)
  Pallas kernels  8.18 us (11%)
    all_to_all x1, blocking collectives, on_device(): mine = lax.all_to_all(data, ('zh', 'y'), 0, 0, tiled=True)  38 us
    all_to_all x1, blocking collectives, on_device(): scaled = lax.all_to_all(scaled, ('x', 'zl'), 0, 0, tiled=True)  8.07 us
    all_to_all x1, waiting for transfers between devices, on_device(): slabs = lax.all_to_all(slabs, ('x', 'zl'), 0, 0, tiled=True)  7.8 us
    ppermute x1, starting transfers between devices, on_device(): other = lax.ppermute(mine, 'core', [(0, 1), (1, 0)])  6.73 us
    all_to_all x1, starting transfers between devices, on_device(): slabs = lax.all_to_all(slabs, ('x', 'zl'), 0, 0, tiled=True)  5.83 us
    pallas_call x1, Pallas kernels, local_dft(): pl.pallas_call(local_dft_kernel, in_specs=[SMEM, VMEM, VMEM, VMEM, VMEM],...  3.26 us
    ppermute x1, waiting for transfers between devices, on_device(): other = lax.ppermute(mine, 'core', [(0, 1), (1, 0)])  1.55 us
  transfers between devices with their start and end apart: 2, of which 2 were waited for; matrix products, arithmetic and copies ran while one was open for 0% of the time, Pallas kernels for 2%

profile of v6, /device:TPU:9, one launch (start us, length us, event | category | flops | bytes accessed | tf_op | source)
XLA Modules:
  0.0 76.3 jit_solution(8013252840100208888)
XLA Ops:
  0.0 0.0 copy-start.4
  0.0 0.0 copy-start
  0.0 0.0 copy-start.1
  0.0 0.0 copy-start.2
  0.0 0.0 copy-start.3
  0.0 3.3 %local_dft.1 = bf16[8,4,64,128]{3,2,1,0:T(8,128)(2,1)} custom-call(s32[2,4]{1,0:T(2,128)} %bitcast.5, bf16[6,8,64,128]{3,2,1,0:T(8,128)(2,1)} %val.1, bf16[6,8,64,128]{3,2,1,0:T(8,128)(2,1)} %cond.1, bf16[256,256]{1,0:T(8,128)(2,1)} %constant.6.clone.z_tab, bf16[64,128]{1,0:T(8,128)(2,1)} %constant.7.clone.y_tab), custom_call_target="tpu_custom_call" | custom-call | tf_op jit(solution)/shard_map/local_dft/pallas_call | solution.py:96
  3.3 5.8 %all-to-all-start = ((bf16[8,4,64,128]{3,2,1,0:T(8,128)(2,1)}), bf16[8,4,64,128]{3,2,1,0:T(8,128)(2,1)S(1)}, u32[]{:S(2)}, u32[]{:S(2)}) async-start(bf16[8,4,64,128]{3,2,1,0:T(8,128)(2,1)} %local_dft.1), calls=%async_computation | async-start | bytes 1048576 | tf_op jit(solution)/shard_map/all_to_all | solution.py:252
  9.1 0.0 copy-done.4
  9.1 0.0 copy-done
  9.1 0.0 copy-done.1
  9.2 0.0 copy-done.2
  9.2 0.0 copy-done.3
  9.2 1.4 %picks.1 = (bf16[512,1280]{1,0:T(8,128)(2,1)S(1)}, f32[256,1280]{1,0:T(8,128)S(1)}, f32[8,256]{1,0:T(8,128)S(1)}) custom-call(s32[2,4]{1,0:T(2,128)S(1)} %bitcast.6, f32[6]{0:T(128)S(1)} %copy-done.2, f32[6]{0:T(128)S(1)} %copy-done.3, s32[1,1280]{1,0:T(1,128)S(1)} %reshape.9.g_map, bf16[256,128]{1,0:T(8,128)(2,1)S(1)} %copy-done), custom_call_target="tpu_custom_call" | custom-call | tf_op jit(solution)/shard_map/picks/pallas_call | solution.py:121
  10.6 7.8 %all-to-all-done.slabs = bf16[8,4,64,128]{3,2,1,0:T(8,128)(2,1)S(1)} async-done(((bf16[8,4,64,128]{3,2,1,0:T(8,128)(2,1)}), bf16[8,4,64,128]{3,2,1,0:T(8,128)(2,1)S(1)}, u32[]{:S(2)}, u32[]{:S(2)}) %all-to-all-start) | async-done | bytes 524320 | tf_op jit(solution)/shard_map/all_to_all | solution.py:252
  18.4 0.9 %elements.1 = (bf16[8,1280]{1,0:T(8,128)(2,1)S(1)}, bf16[8,8,1280]{2,1,0:T(8,128)(2,1)S(1)}) custom-call(bf16[8,4,64,128]{3,2,1,0:T(8,128)(2,1)S(1)} %all-to-all-done.slabs, bf16[512,1280]{1,0:T(8,128)(2,1)S(1)} %get-tuple-element.10.column_pick, f32[256,1280]{1,0:T(8,128)S(1)} %get-tuple-element.11.twiddle, f32[8,256]{1,0:T(8,128)S(1)} %get-tuple-element.12.weight), custom_call_target="tpu_custom_call" | custom-call | tf_op jit(solution)/shard_map/elements/pallas_call | solution.py:154
  19.3 8.1 %all_to_all.15.scaled = bf16[8,8,1280]{2,1,0:T(8,128)(2,1)S(1)} all-to-all(bf16[8,8,1280]{2,1,0:T(8,128)(2,1)S(1)} %get-tuple-element.14), channel_id=1, replica_groups=mesh['zh'=4,'y'=8,'core'=2,'x'=4,'zl'=2] {'x','zl'}, dimensions={0} | all-to-all | bytes 327680 | tf_op jit(solution)/shard_map/all_to_all | solution.py:255
  27.4 0.7 messages.1
  28.1 38.0 %all_to_all.16 = bf16[32,8,1664]{2,1,0:T(8,128)(2,1)S(1)} all-to-all(bf16[32,8,1664]{2,1,0:T(8,128)(2,1)S(1)} %messages.1), channel_id=1, replica_groups=mesh['zh'=4,'y'=8,'core'=2,'x'=4,'zl'=2] {'zh','y'}, dimensions={0} | all-to-all | bytes 1703936 | tf_op jit(solution)/shard_map/all_to_all | solution.py:257
  66.1 6.7 %collective-permute-start = (bf16[32,8,1664]{2,1,0:T(8,128)(2,1)S(1)}, bf16[32,8,1664]{2,1,0:T(8,128)(2,1)S(1)}, u32[]{:S(2)}, u32[]{:S(2)}) collective-permute-start(bf16[32,8,1664]{2,1,0:T(8,128)(2,1)S(1)} %all_to_all.16), channel_id=1, source_target_pairs={{0,8},{8,0},{1,9},{9,1},{2,10},{10,2},{3,11},{11,3},{4,12},{12,4},... | collective-permute-start | bytes 2555912 | tf_op jit(solution)/shard_map/ppermute | solution.py:258
  72.9 0.4 first_half.1.start
  73.3 1.6 %collective-permute-done = bf16[32,8,1664]{2,1,0:T(8,128)(2,1)S(1)} collective-permute-done((bf16[32,8,1664]{2,1,0:T(8,128)(2,1)S(1)}, bf16[32,8,1664]{2,1,0:T(8,128)(2,1)S(1)}, u32[]{:S(2)}, u32[]{:S(2)}) %collective-permute-start) | collective-permute-done | bytes 852000 | tf_op jit(solution)/shard_map/ppermute | solution.py:258
  74.8 1.5 %second_half.1 = f32[2,160,1280]{2,1,0:T(8,128)} custom-call(bf16[256,1664]{1,0:T(8,128)(2,1)S(1)} %bitcast.4, f32[320,1280]{1,0:T(8,128)S(1)} %first_half.1.start), custom_call_target="tpu_custom_call" | custom-call | tf_op jit(solution)/shard_map/second_half/pallas_call | solution.py:234
  (1 shorter events, 0.0 us)
Async XLA Ops:
  0.0 9.1 %copy-start.4 = (s32[1280]{0:T(1024)S(1)}, s32[1280]{0:T(1024)}, u32[]{:S(2)}) copy-start(s32[1280]{0:T(1024)} %param.14) | copy-start | bytes 15364
  0.0 9.1 %copy-start = (bf16[256,128]{1,0:T(8,128)(2,1)S(1)}, bf16[256,128]{1,0:T(8,128)(2,1)}, u32[]{:S(2)}) copy-start(bf16[256,128]{1,0:T(8,128)(2,1)} %constant.8.clone.x_tab) | copy-start | bytes 196612
  0.0 9.1 %copy-start.1 = (s32[4,2]{0,1:T(2,128)S(1)}, s32[4,2]{0,1:T(2,128)}, u32[]{:S(2)}) copy-start(s32[4,2]{0,1:T(2,128)} %param.11) | copy-start | bytes 100
  0.0 9.2 %copy-start.2 = (f32[6]{0:T(128)S(1)}, f32[6]{0:T(128)}, u32[]{:S(2)}) copy-start(f32[6]{0:T(128)} %e_val.1) | copy-start | bytes 76
  0.0 9.2 %copy-start.3 = (f32[6]{0:T(128)S(1)}, f32[6]{0:T(128)}, u32[]{:S(2)}) copy-start(f32[6]{0:T(128)} %e_cond.1) | copy-start | bytes 76
  3.3 15.1 %all-to-all-start = ((bf16[8,4,64,128]{3,2,1,0:T(8,128)(2,1)}), bf16[8,4,64,128]{3,2,1,0:T(8,128)(2,1)S(1)}, u32[]{:S(2)}, u32[]{:S(2)}) async-start(bf16[8,4,64,128]{3,2,1,0:T(8,128)(2,1)} %local_dft.1), calls=%async_computation | async-start | bytes 1048576 | tf_op jit(solution)/shard_map/all_to_all | solution.py:252
  66.1 8.7 %collective-permute-start = (bf16[32,8,1664]{2,1,0:T(8,128)(2,1)S(1)}, bf16[32,8,1664]{2,1,0:T(8,128)(2,1)S(1)}, u32[]{:S(2)}, u32[]{:S(2)}) collective-permute-start(bf16[32,8,1664]{2,1,0:T(8,128)(2,1)S(1)} %all_to_all.16), channel_id=1, source_target_pairs={{0,8},{8,0},{1,9},{9,1},{2,10},{10,2},{3,11},{11,3},{4,12},{12,4},... | collective-permute-start | bytes 2555912 | tf_op jit(solution)/shard_map/ppermute | solution.py:258

commit v7 on v6

--- a/solution.py
+++ b/solution.py
@@ -53,7 +53,7 @@
 ANY = pl.BlockSpec(memory_space=pl.ANY)
 
 
-def local_dft_kernel(bands, val, cond, z_tab, y_tab, out, scratch):
+def local_dft_kernel(bands, val, cond, z_tab, y_tab, out, scratch, stage, sems):
     first = lax.broadcasted_iota(jnp.int32, (N // 2, 2 * N), 1) < N
 
     def along_z(i):
@@ -82,23 +82,33 @@
         base = i * 16 * PITCH
         for k in range(N // 2):
             rows = scratch[pl.ds(base + k, 16, stride=PITCH), :]
-            out[k // 4, k % 4, pl.ds(16 * i, 16), :] = rows.astype(BF16)
-
+            stage[k // 4, k % 4, pl.ds(16 * i, 16), :] = rows.astype(BF16)
+        part = (slice(None), slice(None), pl.ds(16 * i, 16))
+        copies.append(pltpu.make_async_copy(stage.at[part], out.at[part], sems.at[i]))
+        copies[-1].start()
+
+    copies = []
     mids = [along_z(0)]
     for i in range(4):
         if i < 3:
             mids.append(along_z(i + 1))
         along_y(i, mids[i])
         store(i)
+    for copy in copies:
+        copy.wait()
 
 
 def local_dft(bands, psi_val, psi_cond, z_tab, y_tab):
     return pl.pallas_call(
         local_dft_kernel,
         in_specs=[SMEM, VMEM, VMEM, VMEM, VMEM],
-        out_specs=VMEM,
-        out_shape=pltpu.VMEM((8, 4, N, 2 * N), BF16),
-        scratch_shapes=[pltpu.VMEM((4 * 16 * PITCH, 2 * N), F32)],
+        out_specs=ANY,
+        out_shape=jax.ShapeDtypeStruct((8, 4, N, 2 * N), BF16),
+        scratch_shapes=[
+            pltpu.VMEM((4 * 16 * PITCH, 2 * N), F32),
+            pltpu.VMEM((8, 4, N, 2 * N), BF16),
+            pltpu.SemaphoreType.DMA((4,)),
+        ],
         name="local_dft",
     )(bands, psi_val, psi_cond, z_tab, y_tab)
 

time: 76.6 us -> 76.5 us (level)
  no operation moved by 1% of the time
where the time goes in v7:
time: 76.5 us; the launch traced here: 76.2 us
  blocking collectives  46.1 us (60%)
  starting transfers between devices  12.6 us (16%)
  waiting for transfers between devices  9.36 us (12%)
  Pallas kernels  8.08 us (11%)
    all_to_all x1, blocking collectives, on_device(): mine = lax.all_to_all(data, ('zh', 'y'), 0, 0, tiled=True)  38 us
    all_to_all x1, blocking collectives, on_device(): scaled = lax.all_to_all(scaled, ('x', 'zl'), 0, 0, tiled=True)  8.07 us
    all_to_all x1, waiting for transfers between devices, on_device(): slabs = lax.all_to_all(slabs, ('x', 'zl'), 0, 0, tiled=True)  7.81 us
    ppermute x1, starting transfers between devices, on_device(): other = lax.ppermute(mine, 'core', [(0, 1), (1, 0)])  6.72 us
    all_to_all x1, starting transfers between devices, on_device(): slabs = lax.all_to_all(slabs, ('x', 'zl'), 0, 0, tiled=True)  5.84 us
    pallas_call x1, Pallas kernels, local_dft(): pl.pallas_call(local_dft_kernel, in_specs=[SMEM, VMEM, VMEM, VMEM, VMEM],...  3.16 us
    ppermute x1, waiting for transfers between devices, on_device(): other = lax.ppermute(mine, 'core', [(0, 1), (1, 0)])  1.55 us
  transfers between devices with their start and end apart: 2, of which 2 were waited for; matrix products, arithmetic and copies ran while one was open for 0% of the time, Pallas kernels for 2%

profile of v7, /device:TPU:9, one launch (start us, length us, event | category | flops | bytes accessed | tf_op | source)
XLA Modules:
  0.0 76.2 jit_solution(7628575387422850725)
XLA Ops:
  0.0 0.0 copy-start.4
  0.0 0.0 copy-start
  0.0 0.0 copy-start.1
  0.0 0.0 copy-start.2
  0.0 0.0 copy-start.3
  0.0 3.2 %local_dft.1 = bf16[8,4,64,128]{3,2,1,0:T(8,128)(2,1)} custom-call(s32[2,4]{1,0:T(2,128)} %bitcast.5, bf16[6,8,64,128]{3,2,1,0:T(8,128)(2,1)} %val.1, bf16[6,8,64,128]{3,2,1,0:T(8,128)(2,1)} %cond.1, bf16[256,256]{1,0:T(8,128)(2,1)} %constant.6.clone.z_tab, bf16[64,128]{1,0:T(8,128)(2,1)} %constant.7.clone.y_tab), custom_call_target="tpu_custom_call" | custom-call | tf_op jit(solution)/shard_map/local_dft/pallas_call | solution.py:102
  3.2 5.8 %all-to-all-start = ((bf16[8,4,64,128]{3,2,1,0:T(8,128)(2,1)}), bf16[8,4,64,128]{3,2,1,0:T(8,128)(2,1)S(1)}, u32[]{:S(2)}, u32[]{:S(2)}) async-start(bf16[8,4,64,128]{3,2,1,0:T(8,128)(2,1)} %local_dft.1), calls=%async_computation | async-start | bytes 1048576 | tf_op jit(solution)/shard_map/all_to_all | solution.py:262
  9.0 0.0 copy-done.4
  9.1 0.0 copy-done
  9.1 0.0 copy-done.1
  9.1 0.0 copy-done.2
  9.1 0.0 copy-done.3
  9.1 1.4 %picks.1 = (bf16[512,1280]{1,0:T(8,128)(2,1)S(1)}, f32[256,1280]{1,0:T(8,128)S(1)}, f32[8,256]{1,0:T(8,128)S(1)}) custom-call(s32[2,4]{1,0:T(2,128)S(1)} %bitcast.6, f32[6]{0:T(128)S(1)} %copy-done.2, f32[6]{0:T(128)S(1)} %copy-done.3, s32[1,1280]{1,0:T(1,128)S(1)} %reshape.9.g_map, bf16[256,128]{1,0:T(8,128)(2,1)S(1)} %copy-done), custom_call_target="tpu_custom_call" | custom-call | tf_op jit(solution)/shard_map/picks/pallas_call | solution.py:131
  10.5 7.8 %all-to-all-done.slabs = bf16[8,4,64,128]{3,2,1,0:T(8,128)(2,1)S(1)} async-done(((bf16[8,4,64,128]{3,2,1,0:T(8,128)(2,1)}), bf16[8,4,64,128]{3,2,1,0:T(8,128)(2,1)S(1)}, u32[]{:S(2)}, u32[]{:S(2)}) %all-to-all-start) | async-done | bytes 524320 | tf_op jit(solution)/shard_map/all_to_all | solution.py:262
  18.3 0.9 %elements.1 = (bf16[8,1280]{1,0:T(8,128)(2,1)S(1)}, bf16[8,8,1280]{2,1,0:T(8,128)(2,1)S(1)}) custom-call(bf16[8,4,64,128]{3,2,1,0:T(8,128)(2,1)S(1)} %all-to-all-done.slabs, bf16[512,1280]{1,0:T(8,128)(2,1)S(1)} %get-tuple-element.10.column_pick, f32[256,1280]{1,0:T(8,128)S(1)} %get-tuple-element.11.twiddle, f32[8,256]{1,0:T(8,128)S(1)} %get-tuple-element.12.weight), custom_call_target="tpu_custom_call" | custom-call | tf_op jit(solution)/shard_map/elements/pallas_call | solution.py:164
  19.2 8.1 %all_to_all.15.scaled = bf16[8,8,1280]{2,1,0:T(8,128)(2,1)S(1)} all-to-all(bf16[8,8,1280]{2,1,0:T(8,128)(2,1)S(1)} %get-tuple-element.14), channel_id=1, replica_groups=mesh['zh'=4,'y'=8,'core'=2,'x'=4,'zl'=2] {'x','zl'}, dimensions={0} | all-to-all | bytes 327680 | tf_op jit(solution)/shard_map/all_to_all | solution.py:265
  27.3 0.7 messages.1
  28.0 38.0 %all_to_all.16 = bf16[32,8,1664]{2,1,0:T(8,128)(2,1)S(1)} all-to-all(bf16[32,8,1664]{2,1,0:T(8,128)(2,1)S(1)} %messages.1), channel_id=1, replica_groups=mesh['zh'=4,'y'=8,'core'=2,'x'=4,'zl'=2] {'zh','y'}, dimensions={0} | all-to-all | bytes 1703936 | tf_op jit(solution)/shard_map/all_to_all | solution.py:267
  66.0 6.7 %collective-permute-start = (bf16[32,8,1664]{2,1,0:T(8,128)(2,1)S(1)}, bf16[32,8,1664]{2,1,0:T(8,128)(2,1)S(1)}, u32[]{:S(2)}, u32[]{:S(2)}) collective-permute-start(bf16[32,8,1664]{2,1,0:T(8,128)(2,1)S(1)} %all_to_all.16), channel_id=1, source_target_pairs={{0,8},{8,0},{1,9},{9,1},{2,10},{10,2},{3,11},{11,3},{4,12},{12,4},... | collective-permute-start | bytes 2555912 | tf_op jit(solution)/shard_map/ppermute | solution.py:268
  72.8 0.4 first_half.1.start
  73.2 1.6 %collective-permute-done = bf16[32,8,1664]{2,1,0:T(8,128)(2,1)S(1)} collective-permute-done((bf16[32,8,1664]{2,1,0:T(8,128)(2,1)S(1)}, bf16[32,8,1664]{2,1,0:T(8,128)(2,1)S(1)}, u32[]{:S(2)}, u32[]{:S(2)}) %collective-permute-start) | collective-permute-done | bytes 852000 | tf_op jit(solution)/shard_map/ppermute | solution.py:268
  74.7 1.5 %second_half.1 = f32[2,160,1280]{2,1,0:T(8,128)} custom-call(bf16[256,1664]{1,0:T(8,128)(2,1)S(1)} %bitcast.4, f32[320,1280]{1,0:T(8,128)S(1)} %first_half.1.start), custom_call_target="tpu_custom_call" | custom-call | tf_op jit(solution)/shard_map/second_half/pallas_call | solution.py:244
  (1 shorter events, 0.0 us)
Async XLA Ops:
  0.0 9.0 %copy-start.4 = (s32[1280]{0:T(1024)S(1)}, s32[1280]{0:T(1024)}, u32[]{:S(2)}) copy-start(s32[1280]{0:T(1024)} %param.14) | copy-start | bytes 15364
  0.0 9.1 %copy-start = (bf16[256,128]{1,0:T(8,128)(2,1)S(1)}, bf16[256,128]{1,0:T(8,128)(2,1)}, u32[]{:S(2)}) copy-start(bf16[256,128]{1,0:T(8,128)(2,1)} %constant.8.clone.x_tab) | copy-start | bytes 196612
  0.0 9.1 %copy-start.1 = (s32[4,2]{0,1:T(2,128)S(1)}, s32[4,2]{0,1:T(2,128)}, u32[]{:S(2)}) copy-start(s32[4,2]{0,1:T(2,128)} %param.11) | copy-start | bytes 100
  0.0 9.1 %copy-start.2 = (f32[6]{0:T(128)S(1)}, f32[6]{0:T(128)}, u32[]{:S(2)}) copy-start(f32[6]{0:T(128)} %e_val.1) | copy-start | bytes 76
  0.0 9.1 %copy-start.3 = (f32[6]{0:T(128)S(1)}, f32[6]{0:T(128)}, u32[]{:S(2)}) copy-start(f32[6]{0:T(128)} %e_cond.1) | copy-start | bytes 76
  3.2 15.1 %all-to-all-start = ((bf16[8,4,64,128]{3,2,1,0:T(8,128)(2,1)}), bf16[8,4,64,128]{3,2,1,0:T(8,128)(2,1)S(1)}, u32[]{:S(2)}, u32[]{:S(2)}) async-start(bf16[8,4,64,128]{3,2,1,0:T(8,128)(2,1)} %local_dft.1), calls=%async_computation | async-start | bytes 1048576 | tf_op jit(solution)/shard_map/all_to_all | solution.py:262
  66.0 8.7 %collective-permute-start = (bf16[32,8,1664]{2,1,0:T(8,128)(2,1)S(1)}, bf16[32,8,1664]{2,1,0:T(8,128)(2,1)S(1)}, u32[]{:S(2)}, u32[]{:S(2)}) collective-permute-start(bf16[32,8,1664]{2,1,0:T(8,128)(2,1)S(1)} %all_to_all.16), channel_id=1, source_target_pairs={{0,8},{8,0},{1,9},{9,1},{2,10},{10,2},{3,11},{11,3},{4,12},{12,4},... | collective-permute-start | bytes 2555912 | tf_op jit(solution)/shard_map/ppermute | solution.py:268
